TPU v7x, 32 devices: a whole 2x2x4 slice. The times are simulated.
32 devices in a mesh: seq: 8 (over z, core), grp: 4 (over y, x).
Axes of the slice: x: 2, y: 2, z: 4, core: 2. Of those that a mesh axis runs over, the one named last changes fastest.
Arguments:
- tokens: bfloat16 [65536, 1280], P(('seq', 'grp')), may hold values from -27 to 27
- slot_keys: bfloat16 [1280, 128], replicated, may hold values from -1.5 to 1.5
- norm_gain: float32 [32, 1280], P(('seq', 'grp')), may hold values from 0.1 to 1.9
- w_in: bfloat16 [32, 1280, 2560], P(('seq', 'grp')), may hold values from -0.15625 to 0.15625
- w_out: bfloat16 [32, 2560, 1280], P(('seq', 'grp')), may hold values from -0.125 to 0.125
Outputs:
- mixed: bfloat16 [65536, 1280], P(('seq', 'grp'))
All inputs are finite; a program needn't handle non-finite values.
Results may differ from a plain program's by a relative error of at most 0.007.
Values may be sent and summed in bfloat16 or wider, within the bound.
No kernel may reach another device: no remote copies, remote signals or barrier semaphores. Data moves between devices by JAX's collectives and lax.ppermute only.
A program may use at most 128 MiB of HBM per device.

v0:
```python
import jax
import jax.numpy as jnp
from jax import lax
from jax.sharding import PartitionSpec as P


def on_device(tokens, slot_keys, norm_gain, w_in, w_out):
    devices = lax.axis_size(("seq", "grp"))
    logits = jnp.dot(tokens, slot_keys, preferred_element_type=jnp.float32)
    per_dev = logits.shape[1] // devices
    maxima = jnp.max(logits, axis=0)
    scores = jnp.exp(logits - maxima[None, :])
    totals = jnp.sum(scores, axis=0)
    weights = scores.astype(jnp.bfloat16)
    dims = (((0,), (0,)), ((), ()))
    numer_local = lax.dot_general(weights, tokens, dims, preferred_element_type=jnp.float32)
    parts, peaks, sums = (
        lax.all_to_all(numer_local, ("seq", "grp"), split_axis=0, concat_axis=0, tiled=True),
        lax.all_to_all(maxima, ("seq", "grp"), split_axis=0, concat_axis=0, tiled=True),
        lax.all_to_all(totals, ("seq", "grp"), split_axis=0, concat_axis=0, tiled=True),
    )
    peaks = peaks.reshape(devices, per_dev)
    factor = jnp.exp(peaks - jnp.max(peaks, axis=0, keepdims=True))
    numer = jnp.sum(parts.reshape(devices, per_dev, -1) * factor[:, :, None], axis=0)
    own_total = jnp.sum(sums.reshape(devices, per_dev) * factor, axis=0)
    slot_in = numer / own_total[:, None]
    normed = (slot_in * norm_gain[0][None, :]).astype(jnp.bfloat16)
    hidden = jax.nn.gelu(jnp.dot(normed, w_in[0], preferred_element_type=jnp.float32)).astype(
        jnp.bfloat16
    )
    expert_out = jnp.dot(hidden, w_out[0], preferred_element_type=jnp.float32).astype(jnp.bfloat16)
    row_top = jnp.max(logits, axis=1, keepdims=True)
    row_exp = jnp.exp(logits - row_top)
    combine = (row_exp / jnp.sum(row_exp, axis=1, keepdims=True)).astype(jnp.bfloat16)
    gathered = lax.all_gather(expert_out, ("seq", "grp"), axis=0, tiled=True)
    mixed = jnp.dot(combine, gathered, preferred_element_type=jnp.float32)
    return mixed.astype(jnp.bfloat16)


def solution(mesh):
    return jax.shard_map(
        on_device,
        mesh=mesh,
        in_specs=(
            P(("seq", "grp"), None),
            P(),
            P(("seq", "grp"), None),
            P(("seq", "grp"), None, None),
            P(("seq", "grp"), None, None),
        ),
        out_specs=P(("seq", "grp"), None),
        check_vma=False,
    )
```

profile of v0, /device:TPU:0, one launch (start us, length us, event | category | flops | bytes accessed | tf_op | source)
XLA Modules:
  0.0 129.9 jit_solution(6131586817786573005)
XLA Ops:
  0.0 0.0 copy-start
  0.0 1.0 copy-done
  1.0 4.1 %fusion.47 = (f32[2048]{0:T(1024)S(1)}, f32[128]{0:T(128)S(1)}, f32[2048,128]{1,0:T(8,128)S(1)}) fusion(bf16[2048,1280]{1,0:T(8,128)(2,1)} %param.5, bf16[1280,128]{1,0:T(8,128)(2,1)S(1)} %copy-done), kind=kOutput, calls=%fused_computation.43 | convolution fusion | flops 671610752 | bytes 6627840 | tf_op jit(solution)/shard_map/dot_general | solution.py:9
  5.1 0.0 copy-start.1
  5.1 0.6 fusion.10
  5.7 0.7 all_to_all.22
  6.4 7.3 %all-to-all-start.2 = ((f32[32,4,1]{1,2,0:T(1,128)}), f32[32,4,1]{1,2,0:T(1,128)S(1)}, u32[]{:S(2)}, u32[]{:S(2)}) async-start(f32[32,4,1]{1,2,0:T(1,128)} %bitcast.2), calls=%async_computation.2 | async-start | bytes 32768 | tf_op jit(solution)/shard_map/all_to_all | solution.py:20
  13.8 0.7 all_to_all.20
  14.5 6.4 %all-to-all-done.2 = f32[32,4,1]{1,2,0:T(1,128)S(1)} async-done(((f32[32,4,1]{1,2,0:T(1,128)}), f32[32,4,1]{1,2,0:T(1,128)S(1)}, u32[]{:S(2)}, u32[]{:S(2)}) %all-to-all-start.2) | async-done | bytes 544 | tf_op jit(solution)/shard_map/all_to_all | solution.py:20
  20.9 2.6 %all-to-all-start.1 = ((f32[32,4,1]{1,2,0:T(1,128)}), f32[32,4,1]{1,2,0:T(1,128)S(1)}, u32[]{:S(2)}, u32[]{:S(2)}) async-start(f32[32,4,1]{1,2,0:T(1,128)} %bitcast), calls=%async_computation.1 | async-start | bytes 32768 | tf_op jit(solution)/shard_map/all_to_all | solution.py:19
  23.4 3.4 %fusion.13 = f32[128,1280]{1,0:T(8,128)S(1)} fusion(bf16[2048,1280]{1,0:T(8,128)(2,1)} %param.5, f32[2048,128]{1,0:T(8,128)S(1)} %get-tuple-element.9, f32[128]{0:T(128)S(1)} %get-tuple-element.8), kind=kOutput, calls=%fused_computation.14 | convolution fusion | flops 671612928 | bytes 6947328 | tf_op jit(solution)/shard_map/dot_general | solution.py:16
  26.9 1.0 all_to_all.18
  27.9 2.8 %all-to-all-done.1 = f32[32,4,1]{1,2,0:T(1,128)S(1)} async-done(((f32[32,4,1]{1,2,0:T(1,128)}), f32[32,4,1]{1,2,0:T(1,128)S(1)}, u32[]{:S(2)}, u32[]{:S(2)}) %all-to-all-start.1) | async-done | bytes 544 | tf_op jit(solution)/shard_map/all_to_all | solution.py:19
  30.6 3.1 %all-to-all-start = ((f32[32,4,1280]{2,1,0:T(4,128)}), f32[32,4,1280]{2,1,0:T(4,128)S(1)}, u32[]{:S(2)}, u32[]{:S(2)}) async-start(f32[32,4,1280]{2,1,0:T(4,128)} %all_to_all.18), calls=%async_computation | async-start | bytes 1310720 | tf_op jit(solution)/shard_map/all_to_all | solution.py:18
  33.7 0.0 copy-done.1
  33.8 0.1 copy.21
  33.8 0.1 reduce_max.29
  33.9 0.1 exponential_bitcast_fusion
  34.0 0.1 copy.22
  34.1 0.1 copy.24
  34.1 0.2 fusion.42
  34.3 18.3 %all-to-all-done = f32[32,4,1280]{2,1,0:T(4,128)S(1)} async-done(((f32[32,4,1280]{2,1,0:T(4,128)}), f32[32,4,1280]{2,1,0:T(4,128)S(1)}, u32[]{:S(2)}, u32[]{:S(2)}) %all-to-all-start) | async-done | bytes 655392 | tf_op jit(solution)/shard_map/all_to_all | solution.py:18
  52.6 0.2 multiply_reduce_fusion
  52.8 6.7 %fusion.7 = bf16[1,4,1280]{2,1,0:T(4,128)(2,1)S(1)} fusion(bf16[1,2560,1280]{2,1,0:T(8,128)(2,1)} %param.9, bf16[1,1280,2560]{2,1,0:T(8,128)(2,1)} %param.8, f32[4,1280]{1,0:T(4,128)S(1)} %multiply_reduce_fusion, f32[1280]{0:T(1024)S(1)} %reduce.1, f32[4]{0:T(128)S(1)} %fusion.42), kind=kOutput, calls=%fused_computation.6 | convolution fusion | flops 52541440 | bytes 13143056 | tf_op jit(solution)/shard_map/dot_general | solution.py:31
  59.5 66.8 %all-gather = bf16[32,4,1280]{2,1,0:T(4,128)(2,1)S(1)} all-gather(bf16[1,4,1280]{2,1,0:T(4,128)(2,1)S(1)} %fusion.7), channel_id=1, replica_groups=mesh['seq'=8,'grp'=4] {'seq','grp'}, dimensions={0}, use_global_device_ids=true | all-gather | bytes 337920 | tf_op jit(solution)/shard_map/all_gather | solution.py:35
  126.3 0.1 reshape.31
  126.3 3.6 %convolution_convert_fusion = bf16[2048,1280]{1,0:T(8,128)(2,1)} fusion(bf16[128,1280]{1,0:T(8,128)(2,1)S(1)} %reshape.31, f32[2048,128]{1,0:T(8,128)S(1)} %get-tuple-element.9, f32[2048]{0:T(1024)S(1)} %get-tuple-element.5, f32[2048]{0:T(1024)S(1)} %get-tuple-element.7), kind=kOutput, calls=%fused_computation | convolution fusion | flops 674496512 | bytes 6635520 | tf_op jit(solution)/shard_map/dot_general | solution.py:36
  (1 shorter events, 0.0 us)
Async XLA Ops:
  0.0 1.0 copy-start
  5.1 28.7 %copy-start.1 = (f32[1,1280]{1,0:T(1,128)S(1)}, f32[1,1280]{1,0:T(1,128)}, u32[]{:S(2)}) copy-start(f32[1,1280]{1,0:T(1,128)} %param.7) | copy-start | bytes 15364
  6.4 14.5 %all-to-all-start.2 = ((f32[32,4,1]{1,2,0:T(1,128)}), f32[32,4,1]{1,2,0:T(1,128)S(1)}, u32[]{:S(2)}, u32[]{:S(2)}) async-start(f32[32,4,1]{1,2,0:T(1,128)} %bitcast.2), calls=%async_computation.2 | async-start | bytes 32768 | tf_op jit(solution)/shard_map/all_to_all | solution.py:20
  20.9 9.8 %all-to-all-start.1 = ((f32[32,4,1]{1,2,0:T(1,128)}), f32[32,4,1]{1,2,0:T(1,128)S(1)}, u32[]{:S(2)}, u32[]{:S(2)}) async-start(f32[32,4,1]{1,2,0:T(1,128)} %bitcast), calls=%async_computation.1 | async-start | bytes 32768 | tf_op jit(solution)/shard_map/all_to_all | solution.py:19
  30.6 21.9 %all-to-all-start = ((f32[32,4,1280]{2,1,0:T(4,128)}), f32[32,4,1280]{2,1,0:T(4,128)S(1)}, u32[]{:S(2)}, u32[]{:S(2)}) async-start(f32[32,4,1280]{2,1,0:T(4,128)} %all_to_all.18), calls=%async_computation | async-start | bytes 1310720 | tf_op jit(solution)/shard_map/all_to_all | solution.py:18
where the time goes:
time: 130 us
  blocking collectives  66.8 us (51%)
  waiting for transfers between devices  27.4 us (21%)
  matrix products  17.8 us (14%)
  starting transfers between devices  13 us (10%)
  local copies, waits for them, and re-layouts  3.74 us (3%)
    all_gather x1, blocking collectives, on_device(): gathered = lax.all_gather(expert_out, ('seq', 'grp'), axis=0, tiled=True)  66.8 us
    all_to_all x1, waiting for transfers between devices, on_device(): lax.all_to_all(numer_local, ('seq', 'grp'), split_axis=0, concat_axis=0,...  18.3 us
    all_to_all x1, starting transfers between devices, on_device(): lax.all_to_all(totals, ('seq', 'grp'), split_axis=0, concat_axis=0, tiled...  7.32 us
    dot_general x1, matrix products, on_device(): jnp.dot(hidden, w_out[0], preferred_element_type=jnp.float32)  6.7 us
    all_to_all x1, waiting for transfers between devices, on_device(): lax.all_to_all(totals, ('seq', 'grp'), split_axis=0, concat_axis=0, tiled...  6.42 us
    dot_general x1, matrix products, on_device(): logits = jnp.dot(tokens, slot_keys, preferred_element_type=jnp.float32)  4.08 us
    dot_general x1, matrix products, on_device(): mixed = jnp.dot(combine, gathered, preferred_element_type=jnp.float32)  3.58 us
    dot_general x1, matrix products, on_device(): lax.dot_general(weights, tokens, dims, preferred_element_type=jnp.float32)  3.4 us
  transfers between devices with their start and end apart: 3, of which 3 were waited for; matrix products, arithmetic and copies ran while one was open for 3% of the time, Pallas kernels for 0%

commit v1 on v0

v1 whole, which is shorter than its diff:
```python
import functools

import jax
import jax.numpy as jnp
from jax import lax
from jax.experimental import pallas as pl
from jax.experimental.pallas import tpu as pltpu
from jax.sharding import PartitionSpec as P

AXES = ("seq", "grp")
LANES = 128
TILE = 256
COLS = 256


def split3(x):
    hi = x.astype(jnp.bfloat16)
    rest = x - hi.astype(jnp.float32)
    mid = rest.astype(jnp.bfloat16)
    low = (rest - mid.astype(jnp.float32)).astype(jnp.bfloat16)
    return hi, mid, low


def dispatch_kernel(devices, tok_hbm, keys_hbm, msg_ref, logits_ref, tok, keys, wt, tok_sem, key_sem):
    rows, width = tok.shape
    slots = keys.shape[1]
    per_dev = slots // devices
    tiles = rows // TILE

    def tok_copy(i):
        part = pl.ds(i * TILE, TILE)
        return pltpu.make_async_copy(tok_hbm.at[part], tok.at[part], tok_sem.at[i])

    key_copy = pltpu.make_async_copy(keys_hbm, keys, key_sem)
    key_copy.start()
    for i in range(tiles):
        tok_copy(i).start()
    key_copy.wait()
    peak8 = jnp.full((8, slots), -jnp.inf, jnp.float32)
    for i in range(tiles):
        tok_copy(i).wait()
        part = pl.ds(i * TILE, TILE)
        logits = jnp.dot(tok[part, :], keys[...], preferred_element_type=jnp.float32)
        logits_ref[part, :] = logits
        peak8 = jnp.maximum(peak8, jnp.max(logits.reshape(TILE // 8, 8, slots), axis=0))
    peak = jnp.max(peak8, axis=0, keepdims=True)
    total8 = jnp.zeros((8, slots), jnp.float32)
    for i in range(tiles):
        part = pl.ds(i * TILE, TILE)
        scores = jnp.exp(logits_ref[part, :] - peak)
        total8 = total8 + jnp.sum(scores.reshape(TILE // 8, 8, slots), axis=0)
        wt[:, part] = scores.astype(jnp.bfloat16).T
    total = jnp.sum(total8, axis=0, keepdims=True)
    for n in range(width // COLS):
        part = pl.ds(n * COLS, COLS)
        numer = jnp.dot(wt[...], tok[:, part], preferred_element_type=jnp.float32)
        for d in range(devices):
            msg_ref[d, :, part] = numer[d * per_dev : (d + 1) * per_dev].astype(jnp.bfloat16)
    stats = [*split3(peak), *split3(total)]
    stats = [s.astype(jnp.float32) for s in stats]
    stats = jnp.concatenate(stats + [jnp.zeros((LANES - len(stats), slots), jnp.float32)], axis=0)
    for b in range(slots // LANES):
        block = stats[:, b * LANES : (b + 1) * LANES].T
        for d in range(LANES // per_dev):
            msg_ref[b * (LANES // per_dev) + d, :, width:] = block[d * per_dev : (d + 1) * per_dev].astype(jnp.bfloat16)


def dispatch(devices, tokens, keys):
    rows, width = tokens.shape
    slots = keys.shape[1]
    per_dev = slots // devices
    return pl.pallas_call(
        functools.partial(dispatch_kernel, devices),
        out_shape=(
            jax.ShapeDtypeStruct((devices, per_dev, width + LANES), jnp.bfloat16),
            jax.ShapeDtypeStruct((rows, slots), jnp.float32),
        ),
        in_specs=[pl.BlockSpec(memory_space=pltpu.HBM)] * 2,
        out_specs=[pl.BlockSpec(memory_space=pltpu.VMEM)] * 2,
        scratch_shapes=[
            pltpu.VMEM((rows, width), jnp.bfloat16),
            pltpu.VMEM(keys.shape, jnp.bfloat16),
            pltpu.VMEM((slots, rows), jnp.bfloat16),
            pltpu.SemaphoreType.DMA((rows // TILE,)),
            pltpu.SemaphoreType.DMA,
        ],
        name="dispatch",
        compiler_params=pltpu.CompilerParams(vmem_limit_bytes=32 << 20),
        cost_estimate=pl.CostEstimate(
            flops=4 * rows * width * slots,
            bytes_accessed=2 * rows * width,
            transcendentals=rows * slots,
        ),
    )(tokens, keys)


def expert_kernel(copies, recv_ref, gain_ref, w_in_hbm, w_out_hbm, out_ref, w_in, w_out, in_sem, out_sem):
    devices, per_dev, wide = recv_ref.shape
    width, hidden = w_in.shape
    step = 512
    n_in, n_out = hidden // step, width // COLS

    def in_copy(i):
        part = pl.ds(i * step, step)
        return pltpu.make_async_copy(w_in_hbm.at[0, :, part], w_in.at[:, part], in_sem.at[i])

    def out_copy(i):
        part = pl.ds(i * step, step)
        return pltpu.make_async_copy(w_out_hbm.at[0, part], w_out.at[part], out_sem.at[i])

    for i in range(n_in):
        in_copy(i).start()
    for i in range(n_in):
        out_copy(i).start()

    stats = recv_ref[:, :, width:].astype(jnp.float32)
    peaks = stats[:, :, 0:1] + stats[:, :, 1:2] + stats[:, :, 2:3]
    totals = stats[:, :, 3:4] + stats[:, :, 4:5] + stats[:, :, 5:6]
    factor = jnp.exp(peaks - jnp.max(peaks, axis=0, keepdims=True))
    own_total = jnp.sum(totals * factor, axis=0)
    numer = jnp.zeros((per_dev, width), jnp.float32)
    for d in range(devices):
        numer = numer + recv_ref[d, :, :width].astype(jnp.float32) * factor[d]
    normed = (numer / own_total * gain_ref[...]).astype(jnp.bfloat16)
    parts = []
    for i in range(n_in):
        in_copy(i).wait()
        parts.append(jnp.dot(normed, w_in[:, i * step : (i + 1) * step], preferred_element_type=jnp.float32))
    acc = jnp.zeros((per_dev, width), jnp.float32)
    for i in range(n_in):
        act = jax.nn.gelu(parts[i]).astype(jnp.bfloat16)
        out_copy(i).wait()
        acc = acc + jnp.dot(act, w_out[i * step : (i + 1) * step, :], preferred_element_type=jnp.float32)
    res = acc.astype(jnp.bfloat16)
    for d in range(copies):
        out_ref[d] = res


def experts(copies, recv, gain, w_in, w_out):
    devices, per_dev, wide = recv.shape
    width, hidden = w_in.shape[1:]
    steps = hidden // 512
    return pl.pallas_call(
        functools.partial(expert_kernel, copies),
        out_shape=jax.ShapeDtypeStruct((copies, per_dev, width), jnp.bfloat16),
        in_specs=[pl.BlockSpec(memory_space=pltpu.VMEM)] * 2 + [pl.BlockSpec(memory_space=pltpu.HBM)] * 2,
        out_specs=pl.BlockSpec(memory_space=pltpu.VMEM),
        scratch_shapes=[
            pltpu.VMEM((width, hidden), jnp.bfloat16),
            pltpu.VMEM((hidden, width), jnp.bfloat16),
            pltpu.SemaphoreType.DMA((steps,)),
            pltpu.SemaphoreType.DMA((steps,)),
        ],
        name="experts",
        compiler_params=pltpu.CompilerParams(vmem_limit_bytes=32 << 20),
        cost_estimate=pl.CostEstimate(
            flops=4 * per_dev * width * hidden,
            bytes_accessed=4 * width * hidden,
            transcendentals=per_dev * hidden,
        ),
    )(recv, gain, w_in, w_out)


def mix_kernel(logits_ref, rows_ref, out_ref, table):
    per_dev = rows_ref.shape[1]

    @pl.when(pl.program_id(0) == 0)
    def _():
        table[...] = rows_ref[...].reshape(table.shape)

    logits = logits_ref[...]
    row_exp = jnp.exp(logits - jnp.max(logits, axis=1, keepdims=True))
    combine = (row_exp / jnp.sum(row_exp, axis=1, keepdims=True)).astype(jnp.bfloat16)
    out_ref[...] = jnp.dot(combine, table[...], preferred_element_type=jnp.float32).astype(jnp.bfloat16)


def mix(logits, gathered):
    rows, slots = logits.shape
    width = gathered.shape[2]
    return pl.pallas_call(
        mix_kernel,
        grid=(rows // TILE,),
        out_shape=jax.ShapeDtypeStruct((rows, width), jnp.bfloat16),
        in_specs=[
            pl.BlockSpec((TILE, slots), lambda i: (i, 0)),
            pl.BlockSpec(gathered.shape, lambda i: (0, 0, 0)),
        ],
        out_specs=pl.BlockSpec((TILE, width), lambda i: (i, 0)),
        scratch_shapes=[pltpu.VMEM((slots, width), jnp.bfloat16)],
        name="mix",
        compiler_params=pltpu.CompilerParams(vmem_limit_bytes=32 << 20),
    )(logits, gathered)


def on_device(tokens, slot_keys, norm_gain, w_in, w_out):
    devices = lax.axis_size(AXES)
    message, logits = dispatch(devices, tokens, slot_keys)
    received = lax.all_to_all(message, AXES, split_axis=0, concat_axis=0, tiled=True)
    copies = experts(devices, received, norm_gain, w_in, w_out)
    gathered = lax.all_to_all(copies, AXES, split_axis=0, concat_axis=0, tiled=True)
    return mix(logits, gathered)


def solution(mesh):
    return jax.shard_map(
        on_device,
        mesh=mesh,
        in_specs=(
            P(AXES, None),
            P(),
            P(AXES, None),
            P(AXES, None, None),
            P(AXES, None, None),
        ),
        out_specs=P(AXES, None),
        check_vma=False,
    )
```

time: 130 us -> 60.1 us (0.46)
  blocking collectives: 66.8 us -> 34.3 us
  waiting for transfers between devices: 27.4 us -> 0 us
  matrix products: 17.8 us -> 0 us
  Pallas kernels: 0 us -> 15.7 us
  starting transfers between devices: 13 us -> 0 us
  local copies, waits for them, and re-layouts: 3.74 us -> 9.87 us
    all_gather x1 -> x0, blocking collectives: 66.8 us -> none  [on_device(): gathered = lax.all_gather(expert_out, ('seq', 'grp'), axis=0, tiled=True)]
    all_to_all x0 -> x2, blocking collectives: none -> 34.3 us  [the longest x1 20.1 us: on_device(): lax.all_to_all(message, AXES, split_axis=0, concat_axis=0, tiled=True)]
    all_to_all x3 -> x0, waiting for transfers between devices: 27.4 us -> none  [the longest x1 18.3 us: on_device(): lax.all_to_all(numer_local, ('seq', 'grp'), split_axis=0, concat_axis=0,...]
    dot_general x4 -> x0, matrix products: 17.8 us -> none  [the longest x1 6.7 us: on_device(): jnp.dot(hidden, w_out[0], preferred_element_type=jnp.float32)]
    pallas_call x0 -> x3, Pallas kernels: none -> 15.7 us  [the longest x1 5.79 us: dispatch(): pl.pallas_call(functools.partial(dispatch_kernel, devices), out_shape=(ja...]
    all_to_all x3 -> x0, starting transfers between devices: 13 us -> none  [the longest x1 7.32 us: on_device(): lax.all_to_all(totals, ('seq', 'grp'), split_axis=0, concat_axis=0, tiled...]
    unnamed x5 -> x10, local copies, waits for them, and re-layouts: 1.06 us -> 9.87 us
    all_to_all x5 -> x0, local copies, waits for them, and re-layouts: 2.59 us -> none  [the longest x1 1.02 us: on_device(): lax.all_to_all(numer_local, ('seq', 'grp'), split_axis=0, concat_axis=0,...]
  transfers between devices with their start and end apart: 3 -> 0, of which waited for: 3 -> 0; matrix products, arithmetic and copies ran while one was open for 3% -> 0% of each run, Pallas kernels for 0% -> 0%
where the time goes in v1:
time: 60.1 us; the launch traced here: 59.8 us
  blocking collectives  34.3 us (57%)
  Pallas kernels  15.7 us (26%)
  local copies, waits for them, and re-layouts  9.87 us (16%)
    all_to_all x1, blocking collectives, on_device(): lax.all_to_all(message, AXES, split_axis=0, concat_axis=0, tiled=True)  20.1 us
    all_to_all x1, blocking collectives, on_device(): lax.all_to_all(copies, AXES, split_axis=0, concat_axis=0, tiled=True)  14.2 us
    unnamed x10, local copies, waits for them, and re-layouts  9.87 us
    pallas_call x1, Pallas kernels, dispatch(): pl.pallas_call(functools.partial(dispatch_kernel, devices), out_shape=(ja...  5.79 us
    pallas_call x1, Pallas kernels, mix(): pl.pallas_call(mix_kernel, grid=(rows // TILE,), out_shape=jax.ShapeDtype...  5.78 us
    pallas_call x1, Pallas kernels, experts(): pl.pallas_call(functools.partial(expert_kernel, copies), out_shape=jax.Sh...  4.08 us

profile of v1, /device:TPU:0, one launch (start us, length us, event | category | flops | bytes accessed | tf_op | source)
XLA Modules:
  0.0 59.8 jit_solution(13375555666152096177)
XLA Ops:
  0.0 0.0 copy-start.2
  0.0 2.5 %copy-done.2 = bf16[2048,1280]{1,0:T(8,128)(2,1)S(1)} copy-done((bf16[2048,1280]{1,0:T(8,128)(2,1)S(1)}, bf16[2048,1280]{1,0:T(8,128)(2,1)}, u32[]{:S(2)}) %copy-start.2) | copy-done | bytes 5242904
  2.5 0.0 copy-start.3
  2.5 1.0 %copy-done.3 = bf16[1280,128]{1,0:T(8,128)(2,1)S(1)} copy-done((bf16[1280,128]{1,0:T(8,128)(2,1)S(1)}, bf16[1280,128]{1,0:T(8,128)(2,1)}, u32[]{:S(2)}) %copy-start.3) | copy-done | bytes 327704
  3.5 5.8 %dispatch.1 = (bf16[32,4,1408]{2,1,0:T(4,128)(2,1)S(1)}, f32[2048,128]{1,0:T(8,128)S(1)}) custom-call(bf16[2048,1280]{1,0:T(8,128)(2,1)S(1)} %copy-done.2, bf16[1280,128]{1,0:T(8,128)(2,1)S(1)} %copy-done.3), custom_call_target="tpu_custom_call" | custom-call | flops 1342177280 | bytes 5242880 | tf_op jit(solution)/shard_map/dispatch/pallas_call | solution.py:72
  9.3 20.1 %all_to_all.10.recv_ref = bf16[32,4,1408]{2,1,0:T(4,128)(2,1)S(1)} all-to-all(bf16[32,4,1408]{2,1,0:T(4,128)(2,1)S(1)} %get-tuple-element.8), channel_id=1, replica_groups=mesh['seq'=8,'grp'=4] {'seq','grp'}, dimensions={0} | all-to-all | bytes 720896 | tf_op jit(solution)/shard_map/all_to_all | solution.py:198
  29.3 0.0 copy-start
  29.3 2.9 %copy-done = bf16[1,1280,2560]{2,1,0:T(8,128)(2,1)S(1)} copy-done((bf16[1,1280,2560]{2,1,0:T(8,128)(2,1)S(1)}, bf16[1,1280,2560]{2,1,0:T(8,128)(2,1)}, u32[]{:S(2)}) %copy-start) | copy-done | bytes 6553624
  32.2 0.0 copy-start.1
  32.2 2.9 %copy-done.1 = bf16[1,2560,1280]{2,1,0:T(8,128)(2,1)S(1)} copy-done((bf16[1,2560,1280]{2,1,0:T(8,128)(2,1)S(1)}, bf16[1,2560,1280]{2,1,0:T(8,128)(2,1)}, u32[]{:S(2)}) %copy-start.1) | copy-done | bytes 6553624
  35.0 0.0 copy-start.4
  35.0 0.7 %copy-done.4 = f32[1,1280]{1,0:T(1,128)S(1)} copy-done((f32[1,1280]{1,0:T(1,128)S(1)}, f32[1,1280]{1,0:T(1,128)}, u32[]{:S(2)}) %copy-start.4) | copy-done | bytes 5144
  35.7 4.1 %experts.1 = bf16[32,4,1280]{2,1,0:T(4,128)(2,1)S(1)} custom-call(bf16[32,4,1408]{2,1,0:T(4,128)(2,1)S(1)} %all_to_all.10.recv_ref, f32[1,1280]{1,0:T(1,128)S(1)} %copy-done.4, bf16[1,1280,2560]{2,1,0:T(8,128)(2,1)S(1)} %copy-done, bf16[1,2560,1280]{2,1,0:T(8,128)(2,1)S(1)} %copy-done.1), custom_call_target="tpu_custom_call" | custom-call | flops 52428800 | bytes 13107200 | tf_op jit(solution)/shard_map/experts/pallas_call | solution.py:143
  39.8 14.2 %all_to_all.11.rows_ref = bf16[32,4,1280]{2,1,0:T(4,128)(2,1)S(1)} all-to-all(bf16[32,4,1280]{2,1,0:T(4,128)(2,1)S(1)} %experts.1), channel_id=1, replica_groups=mesh['seq'=8,'grp'=4] {'seq','grp'}, dimensions={0} | all-to-all | bytes 655360 | tf_op jit(solution)/shard_map/all_to_all | solution.py:200
  54.0 5.8 %mix.1 = bf16[2048,1280]{1,0:T(8,128)(2,1)} custom-call(f32[2048,128]{1,0:T(8,128)S(1)} %get-tuple-element.7.logits_ref, bf16[32,4,1280]{2,1,0:T(4,128)(2,1)S(1)} %all_to_all.11.rows_ref), custom_call_target="tpu_custom_call" | custom-call | tf_op jit(solution)/shard_map/mix/pallas_call | solution.py:180
Async XLA Ops:
  0.0 2.5 %copy-start.2 = (bf16[2048,1280]{1,0:T(8,128)(2,1)S(1)}, bf16[2048,1280]{1,0:T(8,128)(2,1)}, u32[]{:S(2)}) copy-start(bf16[2048,1280]{1,0:T(8,128)(2,1)} %tok_hbm.1) | copy-start | bytes 15728644
  2.5 1.0 %copy-start.3 = (bf16[1280,128]{1,0:T(8,128)(2,1)S(1)}, bf16[1280,128]{1,0:T(8,128)(2,1)}, u32[]{:S(2)}) copy-start(bf16[1280,128]{1,0:T(8,128)(2,1)} %keys_hbm.1) | copy-start | bytes 983044
  29.3 2.9 %copy-start = (bf16[1,1280,2560]{2,1,0:T(8,128)(2,1)S(1)}, bf16[1,1280,2560]{2,1,0:T(8,128)(2,1)}, u32[]{:S(2)}) copy-start(bf16[1,1280,2560]{2,1,0:T(8,128)(2,1)} %w_in_hbm.1) | copy-start | bytes 19660804
  32.2 2.9 %copy-start.1 = (bf16[1,2560,1280]{2,1,0:T(8,128)(2,1)S(1)}, bf16[1,2560,1280]{2,1,0:T(8,128)(2,1)}, u32[]{:S(2)}) copy-start(bf16[1,2560,1280]{2,1,0:T(8,128)(2,1)} %w_out_hbm.1) | copy-start | bytes 19660804
  35.0 0.7 %copy-start.4 = (f32[1,1280]{1,0:T(1,128)S(1)}, f32[1,1280]{1,0:T(1,128)}, u32[]{:S(2)}) copy-start(f32[1,1280]{1,0:T(1,128)} %gain_ref.1) | copy-start | bytes 15364

commit v2 on v1

--- a/solution.py
+++ b/solution.py
@@ -11,6 +11,12 @@
 LANES = 128
 TILE = 256
 COLS = 256
+DEPTH = 640
+CHUNK = 1024
+
+
+def in_hbm(x):
+    return pltpu.with_memory_space_constraint(x, pltpu.HBM)
 
 
 def split3(x):
@@ -26,19 +32,21 @@
     slots = keys.shape[1]
     per_dev = slots // devices
     tiles = rows // TILE
+    chunks = rows // CHUNK
 
     def tok_copy(i):
-        part = pl.ds(i * TILE, TILE)
+        part = pl.ds(i * CHUNK, CHUNK)
         return pltpu.make_async_copy(tok_hbm.at[part], tok.at[part], tok_sem.at[i])
 
     key_copy = pltpu.make_async_copy(keys_hbm, keys, key_sem)
     key_copy.start()
-    for i in range(tiles):
+    for i in range(chunks):
         tok_copy(i).start()
     key_copy.wait()
     peak8 = jnp.full((8, slots), -jnp.inf, jnp.float32)
     for i in range(tiles):
-        tok_copy(i).wait()
+        if i * TILE % CHUNK == 0:
+            tok_copy(i * TILE // CHUNK).wait()
         part = pl.ds(i * TILE, TILE)
         logits = jnp.dot(tok[part, :], keys[...], preferred_element_type=jnp.float32)
         logits_ref[part, :] = logits
@@ -81,7 +89,7 @@
             pltpu.VMEM((rows, width), jnp.bfloat16),
             pltpu.VMEM(keys.shape, jnp.bfloat16),
             pltpu.VMEM((slots, rows), jnp.bfloat16),
-            pltpu.SemaphoreType.DMA((rows // TILE,)),
+            pltpu.SemaphoreType.DMA((rows // CHUNK,)),
             pltpu.SemaphoreType.DMA,
         ],
         name="dispatch",
@@ -91,26 +99,49 @@
             bytes_accessed=2 * rows * width,
             transcendentals=rows * slots,
         ),
-    )(tokens, keys)
-
-
-def expert_kernel(copies, recv_ref, gain_ref, w_in_hbm, w_out_hbm, out_ref, w_in, w_out, in_sem, out_sem):
+    )(in_hbm(tokens), in_hbm(keys))
+
+
+def combine_kernel(logits_ref, combine_ref):
+    for i in range(logits_ref.shape[0] // TILE):
+        part = pl.ds(i * TILE, TILE)
+        logits = logits_ref[part, :]
+        row_exp = jnp.exp(logits - jnp.max(logits, axis=1, keepdims=True))
+        combine_ref[part, :] = (row_exp / jnp.sum(row_exp, axis=1, keepdims=True)).astype(jnp.bfloat16)
+
+
+def combining(logits):
+    return pl.pallas_call(
+        combine_kernel,
+        out_shape=jax.ShapeDtypeStruct(logits.shape, jnp.bfloat16),
+        in_specs=[pl.BlockSpec(memory_space=pltpu.VMEM)],
+        out_specs=pl.BlockSpec(memory_space=pltpu.VMEM),
+        name="combining",
+        compiler_params=pltpu.CompilerParams(vmem_limit_bytes=32 << 20),
+        cost_estimate=pl.CostEstimate(
+            flops=8 * logits.size, bytes_accessed=6 * logits.size, transcendentals=logits.size
+        ),
+    )(logits)
+
+
+def expert_kernel(copies, recv_ref, gain_hbm, w_in_hbm, w_out_hbm, out_ref, gain, w_in, w_out, gain_sem, in_sem, out_sem):
     devices, per_dev, wide = recv_ref.shape
     width, hidden = w_in.shape
-    step = 512
-    n_in, n_out = hidden // step, width // COLS
+    n_in, n_out = width // DEPTH, hidden // DEPTH
 
     def in_copy(i):
-        part = pl.ds(i * step, step)
-        return pltpu.make_async_copy(w_in_hbm.at[0, :, part], w_in.at[:, part], in_sem.at[i])
+        part = pl.ds(i * DEPTH, DEPTH)
+        return pltpu.make_async_copy(w_in_hbm.at[0, part], w_in.at[part], in_sem.at[i])
 
     def out_copy(i):
-        part = pl.ds(i * step, step)
+        part = pl.ds(i * DEPTH, DEPTH)
         return pltpu.make_async_copy(w_out_hbm.at[0, part], w_out.at[part], out_sem.at[i])
 
+    gain_copy = pltpu.make_async_copy(gain_hbm, gain, gain_sem)
+    gain_copy.start()
     for i in range(n_in):
         in_copy(i).start()
-    for i in range(n_in):
+    for i in range(n_out):
         out_copy(i).start()
 
     stats = recv_ref[:, :, width:].astype(jnp.float32)
@@ -121,16 +152,19 @@
     numer = jnp.zeros((per_dev, width), jnp.float32)
     for d in range(devices):
         numer = numer + recv_ref[d, :, :width].astype(jnp.float32) * factor[d]
-    normed = (numer / own_total * gain_ref[...]).astype(jnp.bfloat16)
-    parts = []
+    gain_copy.wait()
+    normed = (numer / own_total * gain[...]).astype(jnp.bfloat16)
+    pre = jnp.zeros((per_dev, hidden), jnp.float32)
     for i in range(n_in):
+        part = slice(i * DEPTH, (i + 1) * DEPTH)
         in_copy(i).wait()
-        parts.append(jnp.dot(normed, w_in[:, i * step : (i + 1) * step], preferred_element_type=jnp.float32))
+        pre = pre + jnp.dot(normed[:, part], w_in[part, :], preferred_element_type=jnp.float32)
+    act = jax.nn.gelu(pre).astype(jnp.bfloat16)
     acc = jnp.zeros((per_dev, width), jnp.float32)
-    for i in range(n_in):
-        act = jax.nn.gelu(parts[i]).astype(jnp.bfloat16)
+    for i in range(n_out):
+        part = slice(i * DEPTH, (i + 1) * DEPTH)
         out_copy(i).wait()
-        acc = acc + jnp.dot(act, w_out[i * step : (i + 1) * step, :], preferred_element_type=jnp.float32)
+        acc = acc + jnp.dot(act[:, part], w_out[part, :], preferred_element_type=jnp.float32)
     res = acc.astype(jnp.bfloat16)
     for d in range(copies):
         out_ref[d] = res
@@ -139,17 +173,18 @@
 def experts(copies, recv, gain, w_in, w_out):
     devices, per_dev, wide = recv.shape
     width, hidden = w_in.shape[1:]
-    steps = hidden // 512
     return pl.pallas_call(
         functools.partial(expert_kernel, copies),
         out_shape=jax.ShapeDtypeStruct((copies, per_dev, width), jnp.bfloat16),
-        in_specs=[pl.BlockSpec(memory_space=pltpu.VMEM)] * 2 + [pl.BlockSpec(memory_space=pltpu.HBM)] * 2,
+        in_specs=[pl.BlockSpec(memory_space=pltpu.VMEM)] + [pl.BlockSpec(memory_space=pltpu.HBM)] * 3,
         out_specs=pl.BlockSpec(memory_space=pltpu.VMEM),
         scratch_shapes=[
+            pltpu.VMEM(gain.shape, gain.dtype),
             pltpu.VMEM((width, hidden), jnp.bfloat16),
             pltpu.VMEM((hidden, width), jnp.bfloat16),
-            pltpu.SemaphoreType.DMA((steps,)),
-            pltpu.SemaphoreType.DMA((steps,)),
+            pltpu.SemaphoreType.DMA,
+            pltpu.SemaphoreType.DMA((width // DEPTH,)),
+            pltpu.SemaphoreType.DMA((hidden // DEPTH,)),
         ],
         name="experts",
         compiler_params=pltpu.CompilerParams(vmem_limit_bytes=32 << 20),
@@ -158,47 +193,54 @@
             bytes_accessed=4 * width * hidden,
             transcendentals=per_dev * hidden,
         ),
-    )(recv, gain, w_in, w_out)
-
-
-def mix_kernel(logits_ref, rows_ref, out_ref, table):
-    per_dev = rows_ref.shape[1]
-
-    @pl.when(pl.program_id(0) == 0)
-    def _():
-        table[...] = rows_ref[...].reshape(table.shape)
-
-    logits = logits_ref[...]
-    row_exp = jnp.exp(logits - jnp.max(logits, axis=1, keepdims=True))
-    combine = (row_exp / jnp.sum(row_exp, axis=1, keepdims=True)).astype(jnp.bfloat16)
-    out_ref[...] = jnp.dot(combine, table[...], preferred_element_type=jnp.float32).astype(jnp.bfloat16)
-
-
-def mix(logits, gathered):
-    rows, slots = logits.shape
+    )(recv, in_hbm(gain), in_hbm(w_in), in_hbm(w_out))
+
+
+def mix_kernel(combine_ref, rows_ref, out_hbm, table, out, sems):
+    rows, width = out.shape
+    table[...] = rows_ref[...].reshape(table.shape)
+    copies = []
+    for i in range(rows // TILE):
+        part = pl.ds(i * TILE, TILE)
+        for n in range(width // COLS):
+            cols = pl.ds(n * COLS, COLS)
+            mixed = jnp.dot(combine_ref[part, :], table[:, cols], preferred_element_type=jnp.float32)
+            out[part, cols] = mixed.astype(jnp.bfloat16)
+        copies.append(pltpu.make_async_copy(out.at[part], out_hbm.at[part], sems.at[i]))
+        copies[-1].start()
+    for copy in copies:
+        copy.wait()
+
+
+def mix(combine, gathered):
+    rows, slots = combine.shape
     width = gathered.shape[2]
     return pl.pallas_call(
         mix_kernel,
-        grid=(rows // TILE,),
         out_shape=jax.ShapeDtypeStruct((rows, width), jnp.bfloat16),
-        in_specs=[
-            pl.BlockSpec((TILE, slots), lambda i: (i, 0)),
-            pl.BlockSpec(gathered.shape, lambda i: (0, 0, 0)),
+        in_specs=[pl.BlockSpec(memory_space=pltpu.VMEM)] * 2,
+        out_specs=pl.BlockSpec(memory_space=pltpu.HBM),
+        scratch_shapes=[
+            pltpu.VMEM((slots, width), jnp.bfloat16),
+            pltpu.VMEM((rows, width), jnp.bfloat16),
+            pltpu.SemaphoreType.DMA((rows // TILE,)),
         ],
-        out_specs=pl.BlockSpec((TILE, width), lambda i: (i, 0)),
-        scratch_shapes=[pltpu.VMEM((slots, width), jnp.bfloat16)],
         name="mix",
         compiler_params=pltpu.CompilerParams(vmem_limit_bytes=32 << 20),
-    )(logits, gathered)
+        cost_estimate=pl.CostEstimate(
+            flops=2 * rows * slots * width, bytes_accessed=2 * rows * width, transcendentals=0
+        ),
+    )(combine, gathered)
 
 
 def on_device(tokens, slot_keys, norm_gain, w_in, w_out):
     devices = lax.axis_size(AXES)
     message, logits = dispatch(devices, tokens, slot_keys)
     received = lax.all_to_all(message, AXES, split_axis=0, concat_axis=0, tiled=True)
+    combine = combining(logits)
     copies = experts(devices, received, norm_gain, w_in, w_out)
     gathered = lax.all_to_all(copies, AXES, split_axis=0, concat_axis=0, tiled=True)
-    return mix(logits, gathered)
+    return mix(combine, gathered)
 
 
 def solution(mesh):

time: 60.1 us -> 49.2 us (0.82)
  blocking collectives: 34.3 us -> 20.1 us
  waiting for transfers between devices: 0 us -> 11.3 us
  local copies, waits for them, and re-layouts: 9.87 us -> 0 us
  starting transfers between devices: 0 us -> 2.61 us
  Pallas kernels: 15.7 us -> 15 us
    all_to_all x1 -> x0, blocking collectives: 14.2 us -> none  [on_device(): lax.all_to_all(copies, AXES, split_axis=0, concat_axis=0, tiled=True)]
    all_to_all x0 -> x1, waiting for transfers between devices: none -> 11.3 us  [on_device(): lax.all_to_all(copies, AXES, split_axis=0, concat_axis=0, tiled=True)]
    unnamed x10 -> x0, local copies, waits for them, and re-layouts: 9.87 us -> none
    all_to_all x0 -> x1, starting transfers between devices: none -> 2.61 us  [on_device(): lax.all_to_all(copies, AXES, split_axis=0, concat_axis=0, tiled=True)]
    pallas_call x1, Pallas kernels: 4.08 us -> 6.63 us  [experts(): pl.pallas_call(functools.partial(expert_kernel, copies), out_shape=jax.Sh...]
    pallas_call x1 -> x2, Pallas kernels: 5.78 us -> 3.75 us  [the longest x1 2.78 us: mix(): pl.pallas_call(mix_kernel, out_shape=jax.ShapeDtypeStruct((rows, width),...]
    pallas_call x1, Pallas kernels: 5.79 us -> 4.61 us  [dispatch(): pl.pallas_call(functools.partial(dispatch_kernel, devices), out_shape=(ja...]
  transfers between devices with their start and end apart: 0 -> 1, of which waited for: 0 -> 1; matrix products, arithmetic and copies ran while one was open for 0% -> 0% of each run, Pallas kernels for 0% -> 2%
where the time goes in v2:
time: 49.2 us; the launch traced here: 49 us
  blocking collectives  20.1 us (41%)
  Pallas kernels  15 us (30%)
  waiting for transfers between devices  11.3 us (23%)
  starting transfers between devices  2.61 us (5%)
    all_to_all x1, blocking collectives, on_device(): lax.all_to_all(message, AXES, split_axis=0, concat_axis=0, tiled=True)  20.1 us
    all_to_all x1, waiting for transfers between devices, on_device(): lax.all_to_all(copies, AXES, split_axis=0, concat_axis=0, tiled=True)  11.3 us
    pallas_call x1, Pallas kernels, experts(): pl.pallas_call(functools.partial(expert_kernel, copies), out_shape=jax.Sh...  6.63 us
    pallas_call x1, Pallas kernels, dispatch(): pl.pallas_call(functools.partial(dispatch_kernel, devices), out_shape=(ja...  4.61 us
    pallas_call x1, Pallas kernels, mix(): pl.pallas_call(mix_kernel, out_shape=jax.ShapeDtypeStruct((rows, width),...  2.78 us
    all_to_all x1, starting transfers between devices, on_device(): lax.all_to_all(copies, AXES, split_axis=0, concat_axis=0, tiled=True)  2.61 us
  transfers between devices with their start and end apart: 1, of which 1 were waited for; matrix products, arithmetic and copies ran while one was open for 0% of the time, Pallas kernels for 2%

profile of v2, /device:TPU:0, one launch (start us, length us, event | category | flops | bytes accessed | tf_op | source)
XLA Modules:
  0.0 49.0 jit_solution(8210627506146354135)
XLA Ops:
  0.0 4.6 %dispatch.1 = (bf16[32,4,1408]{2,1,0:T(4,128)(2,1)S(1)}, f32[2048,128]{1,0:T(8,128)S(1)}) custom-call(bf16[2048,1280]{1,0:T(8,128)(2,1)} %tok_hbm.1, bf16[1280,128]{1,0:T(8,128)(2,1)} %keys_hbm.1), custom_call_target="tpu_custom_call" | custom-call | flops 1342177280 | bytes 5242880 | tf_op jit(solution)/shard_map/dispatch/pallas_call | solution.py:80
  4.6 20.1 %all_to_all.10.recv_ref = bf16[32,4,1408]{2,1,0:T(4,128)(2,1)S(1)} all-to-all(bf16[32,4,1408]{2,1,0:T(4,128)(2,1)S(1)} %get-tuple-element.8), channel_id=1, replica_groups=mesh['seq'=8,'grp'=4] {'seq','grp'}, dimensions={0} | all-to-all | bytes 720896 | tf_op jit(solution)/shard_map/all_to_all | solution.py:239
  24.7 6.6 %experts.1 = bf16[32,4,1280]{2,1,0:T(4,128)(2,1)} custom-call(bf16[32,4,1408]{2,1,0:T(4,128)(2,1)S(1)} %all_to_all.10.recv_ref, f32[1,1280]{1,0:T(1,128)} %gain_hbm.1, bf16[1,1280,2560]{2,1,0:T(8,128)(2,1)} %w_in_hbm.1, bf16[1,2560,1280]{2,1,0:T(8,128)(2,1)} %w_out_hbm.1), custom_call_target="tpu_custom_call" | custom-call | flops 52428800 | bytes 13107200 | tf_op jit(solution)/shard_map/experts/pallas_call | solution.py:176
  31.3 2.6 %all-to-all-start.1 = ((bf16[32,4,1280]{2,1,0:T(4,128)(2,1)}), bf16[32,4,1280]{2,1,0:T(4,128)(2,1)S(1)}, u32[]{:S(2)}, u32[]{:S(2)}) async-start(bf16[32,4,1280]{2,1,0:T(4,128)(2,1)} %experts.1), calls=%async_computation.1 | async-start | bytes 655360 | tf_op jit(solution)/shard_map/all_to_all | solution.py:242
  33.9 1.0 %combining.1.combine_ref = bf16[2048,128]{1,0:T(8,128)(2,1)S(1)} custom-call(f32[2048,128]{1,0:T(8,128)S(1)} %get-tuple-element.7.logits_ref), custom_call_target="tpu_custom_call" | custom-call | flops 2097152 | bytes 1572864 | tf_op jit(solution)/shard_map/combining/pallas_call | solution.py:114
  34.9 11.3 %all-to-all-done.1.rows_ref = bf16[32,4,1280]{2,1,0:T(4,128)(2,1)S(1)} async-done(((bf16[32,4,1280]{2,1,0:T(4,128)(2,1)}), bf16[32,4,1280]{2,1,0:T(4,128)(2,1)S(1)}, u32[]{:S(2)}, u32[]{:S(2)}) %all-to-all-start.1) | async-done | bytes 327712 | tf_op jit(solution)/shard_map/all_to_all | solution.py:242
  46.2 2.8 %mix.1 = bf16[2048,1280]{1,0:T(8,128)(2,1)} custom-call(bf16[2048,128]{1,0:T(8,128)(2,1)S(1)} %combining.1.combine_ref, bf16[32,4,1280]{2,1,0:T(4,128)(2,1)S(1)} %all-to-all-done.1.rows_ref), custom_call_target="tpu_custom_call" | custom-call | flops 671088640 | bytes 5242880 | tf_op jit(solution)/shard_map/mix/pallas_call | solution.py:218
Async XLA Ops:
  31.3 14.9 %all-to-all-start.1 = ((bf16[32,4,1280]{2,1,0:T(4,128)(2,1)}), bf16[32,4,1280]{2,1,0:T(4,128)(2,1)S(1)}, u32[]{:S(2)}, u32[]{:S(2)}) async-start(bf16[32,4,1280]{2,1,0:T(4,128)(2,1)} %experts.1), calls=%async_computation.1 | async-start | bytes 655360 | tf_op jit(solution)/shard_map/all_to_all | solution.py:242

commit v3 on v2

--- a/solution.py
+++ b/solution.py
@@ -7,7 +7,9 @@
 from jax.experimental.pallas import tpu as pltpu
 from jax.sharding import PartitionSpec as P
 
-AXES = ("seq", "grp")
+SPLIT = ("far", "core", "grp")
+SAME_CORE = ("far", "grp")
+CORES = 2
 LANES = 128
 TILE = 256
 COLS = 256
@@ -27,10 +29,24 @@
     return hi, mid, low
 
 
-def dispatch_kernel(devices, tok_hbm, keys_hbm, msg_ref, logits_ref, tok, keys, wt, tok_sem, key_sem):
+def half_rows(half, slots, groups):
+    size = slots // (CORES * groups)
+    return [pl.ds(pl.multiple_of((g * CORES + half) * size, size), size) for g in range(groups)]
+
+
+def parts_of(peak, total):
+    return [p.astype(jnp.float32) for p in (*split3(peak), *split3(total))]
+
+
+def stats_of(block):
+    peak = block[..., 0:1] + block[..., 1:2] + block[..., 2:3]
+    total = block[..., 3:4] + block[..., 4:5] + block[..., 5:6]
+    return peak, total
+
+
+def dispatch_kernel(groups, tok_hbm, keys_hbm, send_ref, keep_ref, logits_ref, tok, keys, wt, whole, tok_sem, key_sem):
     rows, width = tok.shape
     slots = keys.shape[1]
-    per_dev = slots // devices
     tiles = rows // TILE
     chunks = rows // CHUNK
 
@@ -59,36 +75,41 @@
         total8 = total8 + jnp.sum(scores.reshape(TILE // 8, 8, slots), axis=0)
         wt[:, part] = scores.astype(jnp.bfloat16).T
     total = jnp.sum(total8, axis=0, keepdims=True)
+    stats = parts_of(peak, total)
+    stats = jnp.concatenate(stats + [jnp.zeros((LANES - len(stats), slots), jnp.float32)], axis=0)
+    for b in range(slots // LANES):
+        part = slice(b * LANES, (b + 1) * LANES)
+        whole[part, width:] = stats[:, part].T
     for n in range(width // COLS):
         part = pl.ds(n * COLS, COLS)
-        numer = jnp.dot(wt[...], tok[:, part], preferred_element_type=jnp.float32)
-        for d in range(devices):
-            msg_ref[d, :, part] = numer[d * per_dev : (d + 1) * per_dev].astype(jnp.bfloat16)
-    stats = [*split3(peak), *split3(total)]
-    stats = [s.astype(jnp.float32) for s in stats]
-    stats = jnp.concatenate(stats + [jnp.zeros((LANES - len(stats), slots), jnp.float32)], axis=0)
-    for b in range(slots // LANES):
-        block = stats[:, b * LANES : (b + 1) * LANES].T
-        for d in range(LANES // per_dev):
-            msg_ref[b * (LANES // per_dev) + d, :, width:] = block[d * per_dev : (d + 1) * per_dev].astype(jnp.bfloat16)
-
-
-def dispatch(devices, tokens, keys):
+        whole[:, part] = jnp.dot(wt[...], tok[:, part], preferred_element_type=jnp.float32)
+    core = lax.axis_index("core")
+    size = slots // (CORES * groups)
+    mine, other = half_rows(core, slots, groups), half_rows(1 - core, slots, groups)
+    for g in range(groups):
+        part = pl.ds(g * size, size)
+        send_ref[part, :] = whole[other[g], :].astype(jnp.bfloat16)
+        keep_ref[part, :] = whole[mine[g], :]
+
+
+def dispatch(groups, tokens, keys):
     rows, width = tokens.shape
     slots = keys.shape[1]
-    per_dev = slots // devices
-    return pl.pallas_call(
-        functools.partial(dispatch_kernel, devices),
+    half = slots // CORES
+    return pl.pallas_call(
+        functools.partial(dispatch_kernel, groups),
         out_shape=(
-            jax.ShapeDtypeStruct((devices, per_dev, width + LANES), jnp.bfloat16),
+            jax.ShapeDtypeStruct((half, width + LANES), jnp.bfloat16),
+            jax.ShapeDtypeStruct((half, width + LANES), jnp.float32),
             jax.ShapeDtypeStruct((rows, slots), jnp.float32),
         ),
         in_specs=[pl.BlockSpec(memory_space=pltpu.HBM)] * 2,
-        out_specs=[pl.BlockSpec(memory_space=pltpu.VMEM)] * 2,
+        out_specs=[pl.BlockSpec(memory_space=pltpu.VMEM)] * 3,
         scratch_shapes=[
             pltpu.VMEM((rows, width), jnp.bfloat16),
             pltpu.VMEM(keys.shape, jnp.bfloat16),
             pltpu.VMEM((slots, rows), jnp.bfloat16),
+            pltpu.VMEM((slots, width + LANES), jnp.float32),
             pltpu.SemaphoreType.DMA((rows // CHUNK,)),
             pltpu.SemaphoreType.DMA,
         ],
@@ -100,6 +121,40 @@
             transcendentals=rows * slots,
         ),
     )(in_hbm(tokens), in_hbm(keys))
+
+
+def merge_kernel(keep_ref, got_ref, msg_ref):
+    peers, per_dev, wide = msg_ref.shape
+    width = wide - LANES
+    size = 16
+    lane = lax.broadcasted_iota(jnp.int32, (size, LANES), 1)
+    for b in range(keep_ref.shape[0] // size):
+        rows = pl.ds(b * size, size)
+        keep_peak, keep_total = stats_of(keep_ref[rows, width:])
+        got_peak, got_total = stats_of(got_ref[rows, width:].astype(jnp.float32))
+        peak = jnp.maximum(keep_peak, got_peak)
+        keep_factor, got_factor = jnp.exp(keep_peak - peak), jnp.exp(got_peak - peak)
+        total = keep_factor * keep_total + got_factor * got_total
+        numer = keep_factor * keep_ref[rows, :width] + got_factor * got_ref[rows, :width].astype(jnp.float32)
+        stats = jnp.zeros((size, LANES), jnp.float32)
+        for i, p in enumerate(parts_of(peak, total)):
+            stats = jnp.where(lane == i, p, stats)
+        for d in range(size // per_dev):
+            part = slice(d * per_dev, (d + 1) * per_dev)
+            msg_ref[b * (size // per_dev) + d, :, :width] = numer[part].astype(jnp.bfloat16)
+            msg_ref[b * (size // per_dev) + d, :, width:] = stats[part].astype(jnp.bfloat16)
+
+
+def merge(peers, keep, got):
+    half, wide = keep.shape
+    return pl.pallas_call(
+        merge_kernel,
+        out_shape=jax.ShapeDtypeStruct((peers, half // peers, wide), jnp.bfloat16),
+        in_specs=[pl.BlockSpec(memory_space=pltpu.VMEM)] * 2,
+        out_specs=pl.BlockSpec(memory_space=pltpu.VMEM),
+        name="merge",
+        compiler_params=pltpu.CompilerParams(vmem_limit_bytes=32 << 20),
+    )(keep, got)
 
 
 def combine_kernel(logits_ref, combine_ref):
@@ -124,8 +179,8 @@
     )(logits)
 
 
-def expert_kernel(copies, recv_ref, gain_hbm, w_in_hbm, w_out_hbm, out_ref, gain, w_in, w_out, gain_sem, in_sem, out_sem):
-    devices, per_dev, wide = recv_ref.shape
+def expert_kernel(recv_ref, gain_hbm, w_in_hbm, w_out_hbm, out_ref, gain, w_in, w_out, gain_sem, in_sem, out_sem):
+    peers, per_dev, wide = recv_ref.shape
     width, hidden = w_in.shape
     n_in, n_out = width // DEPTH, hidden // DEPTH
 
@@ -144,13 +199,11 @@
     for i in range(n_out):
         out_copy(i).start()
 
-    stats = recv_ref[:, :, width:].astype(jnp.float32)
-    peaks = stats[:, :, 0:1] + stats[:, :, 1:2] + stats[:, :, 2:3]
-    totals = stats[:, :, 3:4] + stats[:, :, 4:5] + stats[:, :, 5:6]
+    peaks, totals = stats_of(recv_ref[:, :, width:].astype(jnp.float32))
     factor = jnp.exp(peaks - jnp.max(peaks, axis=0, keepdims=True))
     own_total = jnp.sum(totals * factor, axis=0)
     numer = jnp.zeros((per_dev, width), jnp.float32)
-    for d in range(devices):
+    for d in range(peers):
         numer = numer + recv_ref[d, :, :width].astype(jnp.float32) * factor[d]
     gain_copy.wait()
     normed = (numer / own_total * gain[...]).astype(jnp.bfloat16)
@@ -166,16 +219,16 @@
         out_copy(i).wait()
         acc = acc + jnp.dot(act[:, part], w_out[part, :], preferred_element_type=jnp.float32)
     res = acc.astype(jnp.bfloat16)
-    for d in range(copies):
+    for d in range(peers):
         out_ref[d] = res
 
 
-def experts(copies, recv, gain, w_in, w_out):
-    devices, per_dev, wide = recv.shape
+def experts(recv, gain, w_in, w_out):
+    peers, per_dev, wide = recv.shape
     width, hidden = w_in.shape[1:]
     return pl.pallas_call(
-        functools.partial(expert_kernel, copies),
-        out_shape=jax.ShapeDtypeStruct((copies, per_dev, width), jnp.bfloat16),
+        expert_kernel,
+        out_shape=jax.ShapeDtypeStruct((peers, per_dev, width), jnp.bfloat16),
         in_specs=[pl.BlockSpec(memory_space=pltpu.VMEM)] + [pl.BlockSpec(memory_space=pltpu.HBM)] * 3,
         out_specs=pl.BlockSpec(memory_space=pltpu.VMEM),
         scratch_shapes=[
@@ -196,9 +249,15 @@
     )(recv, in_hbm(gain), in_hbm(w_in), in_hbm(w_out))
 
 
-def mix_kernel(combine_ref, rows_ref, out_hbm, table, out, sems):
+def mix_kernel(groups, combine_ref, mine_ref, other_ref, out_hbm, table, out, sems):
     rows, width = out.shape
-    table[...] = rows_ref[...].reshape(table.shape)
+    slots = table.shape[0]
+    core = lax.axis_index("core")
+    for half, ref in ((core, mine_ref), (1 - core, other_ref)):
+        found = ref[...].reshape(slots // CORES, width)
+        size = slots // (CORES * groups)
+        for g, part in enumerate(half_rows(half, slots, groups)):
+            table[part, :] = found[g * size : (g + 1) * size]
     copies = []
     for i in range(rows // TILE):
         part = pl.ds(i * TILE, TILE)
@@ -212,13 +271,13 @@
         copy.wait()
 
 
-def mix(combine, gathered):
+def mix(groups, combine, mine, other):
     rows, slots = combine.shape
-    width = gathered.shape[2]
-    return pl.pallas_call(
-        mix_kernel,
+    width = mine.shape[2]
+    return pl.pallas_call(
+        functools.partial(mix_kernel, groups),
         out_shape=jax.ShapeDtypeStruct((rows, width), jnp.bfloat16),
-        in_specs=[pl.BlockSpec(memory_space=pltpu.VMEM)] * 2,
+        in_specs=[pl.BlockSpec(memory_space=pltpu.VMEM)] * 3,
         out_specs=pl.BlockSpec(memory_space=pltpu.HBM),
         scratch_shapes=[
             pltpu.VMEM((slots, width), jnp.bfloat16),
@@ -230,30 +289,37 @@
         cost_estimate=pl.CostEstimate(
             flops=2 * rows * slots * width, bytes_accessed=2 * rows * width, transcendentals=0
         ),
-    )(combine, gathered)
+    )(combine, mine, other)
 
 
 def on_device(tokens, slot_keys, norm_gain, w_in, w_out):
-    devices = lax.axis_size(AXES)
-    message, logits = dispatch(devices, tokens, slot_keys)
-    received = lax.all_to_all(message, AXES, split_axis=0, concat_axis=0, tiled=True)
+    groups = lax.axis_size("far")
+    peers = lax.axis_size(SAME_CORE)
+    swap = [(0, 1), (1, 0)]
+    send, keep, logits = dispatch(groups, tokens, slot_keys)
+    got = lax.ppermute(send, "core", swap)
     combine = combining(logits)
-    copies = experts(devices, received, norm_gain, w_in, w_out)
-    gathered = lax.all_to_all(copies, AXES, split_axis=0, concat_axis=0, tiled=True)
-    return mix(combine, gathered)
+    message = merge(peers, keep, got)
+    received = lax.all_to_all(message, SAME_CORE, split_axis=0, concat_axis=0, tiled=True)
+    copies = experts(received, norm_gain, w_in, w_out)
+    mine = lax.all_to_all(copies, SAME_CORE, split_axis=0, concat_axis=0, tiled=True)
+    other = lax.ppermute(mine, "core", swap)
+    return mix(groups, combine, mine, other)
 
 
 def solution(mesh):
+    seq, grp = mesh.devices.shape
+    split = jax.sharding.Mesh(mesh.devices.reshape(seq // CORES, CORES, grp), SPLIT)
     return jax.shard_map(
         on_device,
-        mesh=mesh,
+        mesh=split,
         in_specs=(
-            P(AXES, None),
+            P(SPLIT, None),
             P(),
-            P(AXES, None),
-            P(AXES, None, None),
-            P(AXES, None, None),
-        ),
-        out_specs=P(AXES, None),
+            P(SPLIT, None),
+            P(SPLIT, None, None),
+            P(SPLIT, None, None),
+        ),
+        out_specs=P(SPLIT, None),
         check_vma=False,
     )

time: 49.2 us -> 45.6 us (0.927)
  waiting for transfers between devices: 11.3 us -> 1.47 us
  blocking collectives: 20.1 us -> 27.7 us
  starting transfers between devices: 2.61 us -> 0.57 us
  Pallas kernels: 15 us -> 15.6 us
    all_to_all x1 -> x0, waiting for transfers between devices: 11.3 us -> none  [on_device(): lax.all_to_all(copies, AXES, split_axis=0, concat_axis=0, tiled=True)]
    all_to_all x1 -> x2, blocking collectives: 20.1 us -> 27.7 us  [the longest x1 16.4 us: on_device(): lax.all_to_all(message, SAME_CORE, split_axis=0, concat_axis=0, tiled=True)]
    all_to_all x1 -> x0, starting transfers between devices: 2.61 us -> none  [on_device(): lax.all_to_all(copies, AXES, split_axis=0, concat_axis=0, tiled=True)]
    ppermute x0 -> x2, waiting for transfers between devices: none -> 1.47 us  [the longest x1 1.05 us: on_device(): got = lax.ppermute(send, 'core', swap)]
    pallas_call x3 -> x4, Pallas kernels: 14 us -> 14.7 us  [the longest x1 6.81 us: experts(): pl.pallas_call(expert_kernel, out_shape=jax.ShapeDtypeStruct((peers, per_...]
    ppermute x0 -> x2, starting transfers between devices: none -> 0.57 us  [the longest x1 0.56 us: on_device(): got = lax.ppermute(send, 'core', swap)]
  transfers between devices with their start and end apart: 1 -> 2, of which waited for: 1 -> 2; matrix products, arithmetic and copies ran while one was open for 0% -> 0% of each run, Pallas kernels for 2% -> 2%
where the time goes in v3:
time: 45.6 us; the launch traced here: 45.4 us
  blocking collectives  27.7 us (61%)
  Pallas kernels  15.6 us (34%)
  waiting for transfers between devices  1.47 us (3%)
  starting transfers between devices  0.57 us (1%)
    all_to_all x1, blocking collectives, on_device(): lax.all_to_all(message, SAME_CORE, split_axis=0, concat_axis=0, tiled=True)  16.4 us
    all_to_all x1, blocking collectives, on_device(): lax.all_to_all(copies, SAME_CORE, split_axis=0, concat_axis=0, tiled=True)  11.3 us
    pallas_call x1, Pallas kernels, experts(): pl.pallas_call(expert_kernel, out_shape=jax.ShapeDtypeStruct((peers, per_...  6.81 us
    pallas_call x1, Pallas kernels, dispatch(): pl.pallas_call(functools.partial(dispatch_kernel, groups), out_shape=(jax...  4.76 us
    pallas_call x1, Pallas kernels, mix(): pl.pallas_call(functools.partial(mix_kernel, groups), out_shape=jax.Shape...  2.8 us
    ppermute x1, waiting for transfers between devices, on_device(): got = lax.ppermute(send, 'core', swap)  1.05 us
    pallas_call x1, Pallas kernels, combining(): pl.pallas_call(combine_kernel, out_shape=jax.ShapeDtypeStruct(logits.shap...  0.97 us
  transfers between devices with their start and end apart: 2, of which 2 were waited for; matrix products, arithmetic and copies ran while one was open for 0% of the time, Pallas kernels for 2%

profile of v3, /device:TPU:0, one launch (start us, length us, event | category | flops | bytes accessed | tf_op | source)
XLA Modules:
  0.0 45.4 jit_solution(7779048459251658814)
XLA Ops:
  0.0 4.8 %dispatch.1 = (bf16[64,1408]{1,0:T(8,128)(2,1)S(1)}, f32[64,1408]{1,0:T(8,128)S(1)}, f32[2048,128]{1,0:T(8,128)S(1)}) custom-call(bf16[2048,1280]{1,0:T(8,128)(2,1)} %tok_hbm.1, bf16[1280,128]{1,0:T(8,128)(2,1)} %keys_hbm.1), custom_call_target="tpu_custom_call" | custom-call | flops 1342177280 | bytes 5242880 | tf_op jit(solution)/shard_map/dispatch/pallas_call | solution.py:99
  4.8 0.6 %collective-permute-start = (bf16[64,1408]{1,0:T(8,128)(2,1)S(1)}, bf16[64,1408]{1,0:T(8,128)(2,1)S(1)}, u32[]{:S(2)}, u32[]{:S(2)}) collective-permute-start(bf16[64,1408]{1,0:T(8,128)(2,1)S(1)} %get-tuple-element.10), channel_id=1, source_target_pairs={{0,4},{4,0},{1,5},{5,1},{2,6},{6,2},{3,7},{7,3},{8,12},{12,8},{9,1... | collective-permute-start | bytes 540680 | tf_op jit(solution)/shard_map/ppermute | solution.py:300
  5.3 1.0 %collective-permute-done.got_ref = bf16[64,1408]{1,0:T(8,128)(2,1)S(1)} collective-permute-done((bf16[64,1408]{1,0:T(8,128)(2,1)S(1)}, bf16[64,1408]{1,0:T(8,128)(2,1)S(1)}, u32[]{:S(2)}, u32[]{:S(2)}) %collective-permute-start) | collective-permute-done | bytes 180256 | tf_op jit(solution)/shard_map/ppermute | solution.py:300
  6.4 0.3 merge.1
  6.7 16.4 %all_to_all.10.recv_ref = bf16[16,4,1408]{2,1,0:T(4,128)(2,1)S(1)} all-to-all(bf16[16,4,1408]{2,1,0:T(4,128)(2,1)S(1)} %merge.1), channel_id=1, replica_groups=mesh['far'=4,'core'=2,'grp'=4] {'far','grp'}, dimensions={0} | all-to-all | bytes 360448 | tf_op jit(solution)/shard_map/all_to_all | solution.py:303
  23.1 6.8 %experts.1 = bf16[16,4,1280]{2,1,0:T(4,128)(2,1)S(1)} custom-call(bf16[16,4,1408]{2,1,0:T(4,128)(2,1)S(1)} %all_to_all.10.recv_ref, f32[1,1280]{1,0:T(1,128)} %gain_hbm.1, bf16[1,1280,2560]{2,1,0:T(8,128)(2,1)} %w_in_hbm.1, bf16[1,2560,1280]{2,1,0:T(8,128)(2,1)} %w_out_hbm.1), custom_call_target="tpu_custom_call" | custom-call | flops 52428800 | bytes 13107200 | tf_op jit(solution)/shard_map/experts/pallas_call | solution.py:229
  29.9 11.3 %all_to_all.11.mine_ref = bf16[16,4,1280]{2,1,0:T(4,128)(2,1)S(1)} all-to-all(bf16[16,4,1280]{2,1,0:T(4,128)(2,1)S(1)} %experts.1), channel_id=1, replica_groups=mesh['far'=4,'core'=2,'grp'=4] {'far','grp'}, dimensions={0} | all-to-all | bytes 327680 | tf_op jit(solution)/shard_map/all_to_all | solution.py:305
  41.2 0.0 collective-permute-start.1
  41.2 1.0 %combining.1.combine_ref = bf16[2048,128]{1,0:T(8,128)(2,1)S(1)} custom-call(f32[2048,128]{1,0:T(8,128)S(1)} %get-tuple-element.8.logits_ref), custom_call_target="tpu_custom_call" | custom-call | flops 2097152 | bytes 1572864 | tf_op jit(solution)/shard_map/combining/pallas_call | solution.py:169
  42.2 0.4 collective-permute-done.1.other_ref
  42.6 2.8 %mix.1 = bf16[2048,1280]{1,0:T(8,128)(2,1)} custom-call(bf16[2048,128]{1,0:T(8,128)(2,1)S(1)} %combining.1.combine_ref, bf16[16,4,1280]{2,1,0:T(4,128)(2,1)S(1)} %all_to_all.11.mine_ref, bf16[16,4,1280]{2,1,0:T(4,128)(2,1)S(1)} %collective-permute-done.1.other_ref), custom_call_target="tpu_custom_call" | custom-call | flops 671088640 | bytes 5242880 | tf_op jit(solution)/shard_map/mix/pallas_call | solution.py:277
Async XLA Ops:
  4.8 1.6 %collective-permute-start = (bf16[64,1408]{1,0:T(8,128)(2,1)S(1)}, bf16[64,1408]{1,0:T(8,128)(2,1)S(1)}, u32[]{:S(2)}, u32[]{:S(2)}) collective-permute-start(bf16[64,1408]{1,0:T(8,128)(2,1)S(1)} %get-tuple-element.10), channel_id=1, source_target_pairs={{0,4},{4,0},{1,5},{5,1},{2,6},{6,2},{3,7},{7,3},{8,12},{12,8},{9,1... | collective-permute-start | bytes 540680 | tf_op jit(solution)/shard_map/ppermute | solution.py:300
  41.2 1.4 %collective-permute-start.1 = (bf16[16,4,1280]{2,1,0:T(4,128)(2,1)S(1)}, bf16[16,4,1280]{2,1,0:T(4,128)(2,1)S(1)}, u32[]{:S(2)}, u32[]{:S(2)}) collective-permute-start(bf16[16,4,1280]{2,1,0:T(4,128)(2,1)S(1)} %all_to_all.11.mine_ref), channel_id=1, source_target_pairs={{0,4},{4,0},{1,5},{5,1},{2,6},{6,2},{3,7},{7,3},{8,12},{12,8},{9,1... | collective-permute-start | bytes 491528 | tf_op jit(solution)/shard_map/ppermute | solution.py:306

commit v4 on v3

--- a/solution.py
+++ b/solution.py
@@ -13,7 +13,10 @@
 LANES = 128
 TILE = 256
 COLS = 256
-DEPTH = 640
+HEAD = 512
+IN_CHUNKS = (384, 384)
+OUT_CHUNKS = (768, 768, 640, 384)
+STARTS = (4, 2)
 CHUNK = 1024
 
 
@@ -44,7 +47,10 @@
     return peak, total
 
 
-def dispatch_kernel(groups, tok_hbm, keys_hbm, send_ref, keep_ref, logits_ref, tok, keys, wt, whole, tok_sem, key_sem):
+def dispatch_kernel(
+    groups, tok_hbm, keys_hbm, gain_hbm, w_in_hbm, send_ref, keep_ref, logits_ref, gain_ref, head_ref,
+    tok, keys, wt, whole, tok_sem, key_sem, head_sem,
+):
     rows, width = tok.shape
     slots = keys.shape[1]
     tiles = rows // TILE
@@ -59,10 +65,17 @@
     for i in range(chunks):
         tok_copy(i).start()
     key_copy.wait()
+    ahead = (
+        pltpu.make_async_copy(gain_hbm, gain_ref, head_sem.at[0]),
+        pltpu.make_async_copy(w_in_hbm.at[0, pl.ds(0, HEAD)], head_ref, head_sem.at[1]),
+    )
     peak8 = jnp.full((8, slots), -jnp.inf, jnp.float32)
     for i in range(tiles):
         if i * TILE % CHUNK == 0:
             tok_copy(i * TILE // CHUNK).wait()
+            if i == 0:
+                for copy in ahead:
+                    copy.start()
         part = pl.ds(i * TILE, TILE)
         logits = jnp.dot(tok[part, :], keys[...], preferred_element_type=jnp.float32)
         logits_ref[part, :] = logits
@@ -90,9 +103,11 @@
         part = pl.ds(g * size, size)
         send_ref[part, :] = whole[other[g], :].astype(jnp.bfloat16)
         keep_ref[part, :] = whole[mine[g], :]
-
-
-def dispatch(groups, tokens, keys):
+    for copy in ahead:
+        copy.wait()
+
+
+def dispatch(groups, tokens, keys, gain, w_in):
     rows, width = tokens.shape
     slots = keys.shape[1]
     half = slots // CORES
@@ -102,9 +117,11 @@
             jax.ShapeDtypeStruct((half, width + LANES), jnp.bfloat16),
             jax.ShapeDtypeStruct((half, width + LANES), jnp.float32),
             jax.ShapeDtypeStruct((rows, slots), jnp.float32),
-        ),
-        in_specs=[pl.BlockSpec(memory_space=pltpu.HBM)] * 2,
-        out_specs=[pl.BlockSpec(memory_space=pltpu.VMEM)] * 3,
+            jax.ShapeDtypeStruct(gain.shape, gain.dtype),
+            jax.ShapeDtypeStruct((HEAD, w_in.shape[2]), w_in.dtype),
+        ),
+        in_specs=[pl.BlockSpec(memory_space=pltpu.HBM)] * 4,
+        out_specs=[pl.BlockSpec(memory_space=pltpu.VMEM)] * 5,
         scratch_shapes=[
             pltpu.VMEM((rows, width), jnp.bfloat16),
             pltpu.VMEM(keys.shape, jnp.bfloat16),
@@ -112,6 +129,7 @@
             pltpu.VMEM((slots, width + LANES), jnp.float32),
             pltpu.SemaphoreType.DMA((rows // CHUNK,)),
             pltpu.SemaphoreType.DMA,
+            pltpu.SemaphoreType.DMA((2,)),
         ],
         name="dispatch",
         compiler_params=pltpu.CompilerParams(vmem_limit_bytes=32 << 20),
@@ -120,10 +138,10 @@
             bytes_accessed=2 * rows * width,
             transcendentals=rows * slots,
         ),
-    )(in_hbm(tokens), in_hbm(keys))
-
-
-def merge_kernel(keep_ref, got_ref, msg_ref):
+    )(in_hbm(tokens), in_hbm(keys), in_hbm(gain), in_hbm(w_in))
+
+
+def merge_kernel(keep_ref, got_ref, ready_ref, msg_ref):
     peers, per_dev, wide = msg_ref.shape
     width = wide - LANES
     size = 16
@@ -145,32 +163,36 @@
             msg_ref[b * (size // per_dev) + d, :, width:] = stats[part].astype(jnp.bfloat16)
 
 
-def merge(peers, keep, got):
+def merge(peers, keep, got, ready):
     half, wide = keep.shape
     return pl.pallas_call(
         merge_kernel,
         out_shape=jax.ShapeDtypeStruct((peers, half // peers, wide), jnp.bfloat16),
-        in_specs=[pl.BlockSpec(memory_space=pltpu.VMEM)] * 2,
+        in_specs=[pl.BlockSpec(memory_space=pltpu.VMEM)] * 3,
         out_specs=pl.BlockSpec(memory_space=pltpu.VMEM),
         name="merge",
         compiler_params=pltpu.CompilerParams(vmem_limit_bytes=32 << 20),
-    )(keep, got)
-
-
-def combine_kernel(logits_ref, combine_ref):
+    )(keep, got, ready)
+
+
+def combine_kernel(logits_ref, combine_ref, ready_ref):
     for i in range(logits_ref.shape[0] // TILE):
         part = pl.ds(i * TILE, TILE)
         logits = logits_ref[part, :]
         row_exp = jnp.exp(logits - jnp.max(logits, axis=1, keepdims=True))
         combine_ref[part, :] = (row_exp / jnp.sum(row_exp, axis=1, keepdims=True)).astype(jnp.bfloat16)
+    ready_ref[...] = jnp.zeros_like(ready_ref)
 
 
 def combining(logits):
     return pl.pallas_call(
         combine_kernel,
-        out_shape=jax.ShapeDtypeStruct(logits.shape, jnp.bfloat16),
+        out_shape=(
+            jax.ShapeDtypeStruct(logits.shape, jnp.bfloat16),
+            jax.ShapeDtypeStruct((8, LANES), jnp.float32),
+        ),
         in_specs=[pl.BlockSpec(memory_space=pltpu.VMEM)],
-        out_specs=pl.BlockSpec(memory_space=pltpu.VMEM),
+        out_specs=[pl.BlockSpec(memory_space=pltpu.VMEM)] * 2,
         name="combining",
         compiler_params=pltpu.CompilerParams(vmem_limit_bytes=32 << 20),
         cost_estimate=pl.CostEstimate(
@@ -179,25 +201,29 @@
     )(logits)
 
 
-def expert_kernel(recv_ref, gain_hbm, w_in_hbm, w_out_hbm, out_ref, gain, w_in, w_out, gain_sem, in_sem, out_sem):
+def expert_kernel(recv_ref, gain_ref, head_ref, w_in_hbm, w_out_hbm, out_ref, w_in, w_out, in_sem, out_sem):
     peers, per_dev, wide = recv_ref.shape
-    width, hidden = w_in.shape
-    n_in, n_out = width // DEPTH, hidden // DEPTH
-
-    def in_copy(i):
-        part = pl.ds(i * DEPTH, DEPTH)
-        return pltpu.make_async_copy(w_in_hbm.at[0, part], w_in.at[part], in_sem.at[i])
-
-    def out_copy(i):
-        part = pl.ds(i * DEPTH, DEPTH)
-        return pltpu.make_async_copy(w_out_hbm.at[0, part], w_out.at[part], out_sem.at[i])
-
-    gain_copy = pltpu.make_async_copy(gain_hbm, gain, gain_sem)
-    gain_copy.start()
-    for i in range(n_in):
-        in_copy(i).start()
-    for i in range(n_out):
-        out_copy(i).start()
+    width, hidden = w_out.shape[1], w_out.shape[0]
+
+    def spans(sizes):
+        return [(sum(sizes[:i]), size) for i, size in enumerate(sizes)]
+
+    def copy_of(src, dst, sems, i, span, skip):
+        return pltpu.make_async_copy(
+            src.at[0, pl.ds(skip + span[0], span[1])], dst.at[pl.ds(*span)], sems.at[i]
+        )
+
+    in_spans, out_spans = spans(IN_CHUNKS), spans(OUT_CHUNKS)
+    in_copies = [copy_of(w_in_hbm, w_in, in_sem, i, span, HEAD) for i, span in enumerate(in_spans)]
+    out_copies = [copy_of(w_out_hbm, w_out, out_sem, i, span, 0) for i, span in enumerate(out_spans)]
+    waiting = in_copies + out_copies
+    schedule = list(STARTS)
+
+    def start_some():
+        for _ in range(schedule.pop(0) if schedule else 0):
+            waiting.pop(0).start()
+
+    start_some()
 
     peaks, totals = stats_of(recv_ref[:, :, width:].astype(jnp.float32))
     factor = jnp.exp(peaks - jnp.max(peaks, axis=0, keepdims=True))
@@ -205,39 +231,41 @@
     numer = jnp.zeros((per_dev, width), jnp.float32)
     for d in range(peers):
         numer = numer + recv_ref[d, :, :width].astype(jnp.float32) * factor[d]
-    gain_copy.wait()
-    normed = (numer / own_total * gain[...]).astype(jnp.bfloat16)
-    pre = jnp.zeros((per_dev, hidden), jnp.float32)
-    for i in range(n_in):
-        part = slice(i * DEPTH, (i + 1) * DEPTH)
-        in_copy(i).wait()
-        pre = pre + jnp.dot(normed[:, part], w_in[part, :], preferred_element_type=jnp.float32)
+    normed = (numer / own_total * gain_ref[...]).astype(jnp.bfloat16)
+    pre = jnp.dot(normed[:, :HEAD], head_ref[...], preferred_element_type=jnp.float32)
+    for copy, (first, size) in zip(in_copies, in_spans):
+        copy.wait()
+        start_some()
+        pre = pre + jnp.dot(
+            normed[:, HEAD + first : HEAD + first + size],
+            w_in[first : first + size, :],
+            preferred_element_type=jnp.float32,
+        )
     act = jax.nn.gelu(pre).astype(jnp.bfloat16)
     acc = jnp.zeros((per_dev, width), jnp.float32)
-    for i in range(n_out):
-        part = slice(i * DEPTH, (i + 1) * DEPTH)
-        out_copy(i).wait()
+    for copy, (first, size) in zip(out_copies, out_spans):
+        part = slice(first, first + size)
+        copy.wait()
+        start_some()
         acc = acc + jnp.dot(act[:, part], w_out[part, :], preferred_element_type=jnp.float32)
     res = acc.astype(jnp.bfloat16)
     for d in range(peers):
         out_ref[d] = res
 
 
-def experts(recv, gain, w_in, w_out):
+def experts(recv, gain, head, w_in, w_out):
     peers, per_dev, wide = recv.shape
     width, hidden = w_in.shape[1:]
     return pl.pallas_call(
         expert_kernel,
         out_shape=jax.ShapeDtypeStruct((peers, per_dev, width), jnp.bfloat16),
-        in_specs=[pl.BlockSpec(memory_space=pltpu.VMEM)] + [pl.BlockSpec(memory_space=pltpu.HBM)] * 3,
+        in_specs=[pl.BlockSpec(memory_space=pltpu.VMEM)] * 3 + [pl.BlockSpec(memory_space=pltpu.HBM)] * 2,
         out_specs=pl.BlockSpec(memory_space=pltpu.VMEM),
         scratch_shapes=[
-            pltpu.VMEM(gain.shape, gain.dtype),
-            pltpu.VMEM((width, hidden), jnp.bfloat16),
+            pltpu.VMEM((width - HEAD, hidden), jnp.bfloat16),
             pltpu.VMEM((hidden, width), jnp.bfloat16),
-            pltpu.SemaphoreType.DMA,
-            pltpu.SemaphoreType.DMA((width // DEPTH,)),
-            pltpu.SemaphoreType.DMA((hidden // DEPTH,)),
+            pltpu.SemaphoreType.DMA((len(IN_CHUNKS),)),
+            pltpu.SemaphoreType.DMA((len(OUT_CHUNKS),)),
         ],
         name="experts",
         compiler_params=pltpu.CompilerParams(vmem_limit_bytes=32 << 20),
@@ -246,7 +274,7 @@
             bytes_accessed=4 * width * hidden,
             transcendentals=per_dev * hidden,
         ),
-    )(recv, in_hbm(gain), in_hbm(w_in), in_hbm(w_out))
+    )(recv, gain, head, in_hbm(w_in), in_hbm(w_out))
 
 
 def mix_kernel(groups, combine_ref, mine_ref, other_ref, out_hbm, table, out, sems):
@@ -296,12 +324,12 @@
     groups = lax.axis_size("far")
     peers = lax.axis_size(SAME_CORE)
     swap = [(0, 1), (1, 0)]
-    send, keep, logits = dispatch(groups, tokens, slot_keys)
+    send, keep, logits, gain, head = dispatch(groups, tokens, slot_keys, norm_gain, w_in)
     got = lax.ppermute(send, "core", swap)
-    combine = combining(logits)
-    message = merge(peers, keep, got)
+    combine, ready = combining(logits)
+    message = merge(peers, keep, got, ready)
     received = lax.all_to_all(message, SAME_CORE, split_axis=0, concat_axis=0, tiled=True)
-    copies = experts(received, norm_gain, w_in, w_out)
+    copies = experts(received, gain, head, w_in, w_out)
     mine = lax.all_to_all(copies, SAME_CORE, split_axis=0, concat_axis=0, tiled=True)
     other = lax.ppermute(mine, "core", swap)
     return mix(groups, combine, mine, other)

time: 45.6 us -> 43.4 us (0.952)
  Pallas kernels: 15.6 us -> 13.4 us
    pallas_call x1, Pallas kernels: 6.81 us -> 4.57 us  [experts(): pl.pallas_call(expert_kernel, out_shape=jax.ShapeDtypeStruct((peers, per_...]
    ppermute x1, waiting for transfers between devices: 0.42 us -> 1.39 us  [on_device(): other = lax.ppermute(mine, 'core', swap)]
    ppermute x1, waiting for transfers between devices: 1.05 us -> 0.07 us  [on_device(): got = lax.ppermute(send, 'core', swap)]
where the time goes in v4:
time: 43.4 us; the launch traced here: 43.2 us
  blocking collectives  27.7 us (64%)
  Pallas kernels  13.4 us (31%)
  waiting for transfers between devices  1.47 us (3%)
  starting transfers between devices  0.56 us (1%)
    all_to_all x1, blocking collectives, on_device(): lax.all_to_all(message, SAME_CORE, split_axis=0, concat_axis=0, tiled=True)  16.4 us
    all_to_all x1, blocking collectives, on_device(): lax.all_to_all(copies, SAME_CORE, split_axis=0, concat_axis=0, tiled=True)  11.3 us
    pallas_call x1, Pallas kernels, dispatch(): pl.pallas_call(functools.partial(dispatch_kernel, groups), out_shape=(jax...  4.82 us
    pallas_call x1, Pallas kernels, experts(): pl.pallas_call(expert_kernel, out_shape=jax.ShapeDtypeStruct((peers, per_...  4.57 us
    pallas_call x1, Pallas kernels, mix(): pl.pallas_call(functools.partial(mix_kernel, groups), out_shape=jax.Shape...  2.8 us
    ppermute x1, waiting for transfers between devices, on_device(): other = lax.ppermute(mine, 'core', swap)  1.39 us
    pallas_call x1, Pallas kernels, combining(): pl.pallas_call(combine_kernel, out_shape=(jax.ShapeDtypeStruct(logits.sha...  0.97 us
  transfers between devices with their start and end apart: 2, of which 2 were waited for; matrix products, arithmetic and copies ran while one was open for 0% of the time, Pallas kernels for 2%

profile of v4, /device:TPU:0, one launch (start us, length us, event | category | flops | bytes accessed | tf_op | source)
XLA Modules:
  0.0 43.2 jit_solution(17086839382151541853)
XLA Ops:
  0.0 4.8 %dispatch.1 = (bf16[64,1408]{1,0:T(8,128)(2,1)S(1)}, f32[64,1408]{1,0:T(8,128)S(1)}, f32[2048,128]{1,0:T(8,128)S(1)}, f32[1,1280]{1,0:T(1,128)S(1)}, bf16[512,2560]{1,0:T(8,128)(2,1)S(1)}) custom-call(bf16[2048,1280]{1,0:T(8,128)(2,1)} %tok_hbm.1, bf16[1280,128]{1,0:T(8,128)(2,1)} %keys_hbm.1, f32[1,1280]{1,0:T(1,128)} %gain_hbm.1, ...), custom_call_target="tpu_custom_call" | custom-call | flops 1342177280 | bytes 5242880 | tf_op jit(solution)/shard_map/dispatch/pallas_call | solution.py:114
  4.8 0.6 %collective-permute-start = (bf16[64,1408]{1,0:T(8,128)(2,1)S(1)}, bf16[64,1408]{1,0:T(8,128)(2,1)S(1)}, u32[]{:S(2)}, u32[]{:S(2)}) collective-permute-start(bf16[64,1408]{1,0:T(8,128)(2,1)S(1)} %get-tuple-element.15), channel_id=1, source_target_pairs={{0,4},{4,0},{1,5},{5,1},{2,6},{6,2},{3,7},{7,3},{8,12},{12,8},{9,1... | collective-permute-start | bytes 540680 | tf_op jit(solution)/shard_map/ppermute | solution.py:328
  5.4 1.0 %combining.1 = (bf16[2048,128]{1,0:T(8,128)(2,1)S(1)}, f32[8,128]{1,0:T(8,128)S(1)}) custom-call(f32[2048,128]{1,0:T(8,128)S(1)} %get-tuple-element.12.logits_ref), custom_call_target="tpu_custom_call" | custom-call | flops 2097152 | bytes 1572864 | tf_op jit(solution)/shard_map/combining/pallas_call | solution.py:188
  6.4 0.1 collective-permute-done.got_ref
  6.4 0.3 merge.1
  6.7 16.4 %all_to_all.10.recv_ref = bf16[16,4,1408]{2,1,0:T(4,128)(2,1)S(1)} all-to-all(bf16[16,4,1408]{2,1,0:T(4,128)(2,1)S(1)} %merge.1), channel_id=1, replica_groups=mesh['far'=4,'core'=2,'grp'=4] {'far','grp'}, dimensions={0} | all-to-all | bytes 360448 | tf_op jit(solution)/shard_map/all_to_all | solution.py:331
  23.1 4.6 %experts.1 = bf16[16,4,1280]{2,1,0:T(4,128)(2,1)S(1)} custom-call(bf16[16,4,1408]{2,1,0:T(4,128)(2,1)S(1)} %all_to_all.10.recv_ref, f32[1,1280]{1,0:T(1,128)S(1)} %get-tuple-element.17.gain_ref, bf16[512,2560]{1,0:T(8,128)(2,1)S(1)} %get-tuple-element.18.head_ref, bf16[1,1280,2560]{2,1,0:T(8,128)(2,1)} %w_in_hbm.3, bf16[1,2560,1280]{2,1,0:T(8,128)(2,1)} %w_out_hbm.1), custom_call_target="tpu_custom_call" | custom-call | flops 52428800 | bytes 13107200 | tf_op jit(solution)/shard_map/experts/pallas_call | solution.py:259
  27.7 11.3 %all_to_all.11.mine_ref = bf16[16,4,1280]{2,1,0:T(4,128)(2,1)S(1)} all-to-all(bf16[16,4,1280]{2,1,0:T(4,128)(2,1)S(1)} %experts.1), channel_id=1, replica_groups=mesh['far'=4,'core'=2,'grp'=4] {'far','grp'}, dimensions={0} | all-to-all | bytes 327680 | tf_op jit(solution)/shard_map/all_to_all | solution.py:333
  39.0 0.0 collective-permute-start.1
  39.0 1.4 %collective-permute-done.1.other_ref = bf16[16,4,1280]{2,1,0:T(4,128)(2,1)S(1)} collective-permute-done((bf16[16,4,1280]{2,1,0:T(4,128)(2,1)S(1)}, bf16[16,4,1280]{2,1,0:T(4,128)(2,1)S(1)}, u32[]{:S(2)}, u32[]{:S(2)}) %collective-permute-start.1) | collective-permute-done | bytes 163872 | tf_op jit(solution)/shard_map/ppermute | solution.py:334
  40.4 2.8 %mix.1 = bf16[2048,1280]{1,0:T(8,128)(2,1)} custom-call(bf16[2048,128]{1,0:T(8,128)(2,1)S(1)} %get-tuple-element.13.combine_ref, bf16[16,4,1280]{2,1,0:T(4,128)(2,1)S(1)} %all_to_all.11.mine_ref, bf16[16,4,1280]{2,1,0:T(4,128)(2,1)S(1)} %collective-permute-done.1.other_ref), custom_call_target="tpu_custom_call" | custom-call | flops 671088640 | bytes 5242880 | tf_op jit(solution)/shard_map/mix/pallas_call | solution.py:305
Async XLA Ops:
  4.8 1.6 %collective-permute-start = (bf16[64,1408]{1,0:T(8,128)(2,1)S(1)}, bf16[64,1408]{1,0:T(8,128)(2,1)S(1)}, u32[]{:S(2)}, u32[]{:S(2)}) collective-permute-start(bf16[64,1408]{1,0:T(8,128)(2,1)S(1)} %get-tuple-element.15), channel_id=1, source_target_pairs={{0,4},{4,0},{1,5},{5,1},{2,6},{6,2},{3,7},{7,3},{8,12},{12,8},{9,1... | collective-permute-start | bytes 540680 | tf_op jit(solution)/shard_map/ppermute | solution.py:328
  39.0 1.4 %collective-permute-start.1 = (bf16[16,4,1280]{2,1,0:T(4,128)(2,1)S(1)}, bf16[16,4,1280]{2,1,0:T(4,128)(2,1)S(1)}, u32[]{:S(2)}, u32[]{:S(2)}) collective-permute-start(bf16[16,4,1280]{2,1,0:T(4,128)(2,1)S(1)} %all_to_all.11.mine_ref), channel_id=1, source_target_pairs={{0,4},{4,0},{1,5},{5,1},{2,6},{6,2},{3,7},{7,3},{8,12},{12,8},{9,1... | collective-permute-start | bytes 491528 | tf_op jit(solution)/shard_map/ppermute | solution.py:334

commit v5 on v4

--- a/solution.py
+++ b/solution.py
@@ -53,7 +53,6 @@
 ):
     rows, width = tok.shape
     slots = keys.shape[1]
-    tiles = rows // TILE
     chunks = rows // CHUNK
 
     def tok_copy(i):
@@ -69,33 +68,46 @@
         pltpu.make_async_copy(gain_hbm, gain_ref, head_sem.at[0]),
         pltpu.make_async_copy(w_in_hbm.at[0, pl.ds(0, HEAD)], head_ref, head_sem.at[1]),
     )
-    peak8 = jnp.full((8, slots), -jnp.inf, jnp.float32)
-    for i in range(tiles):
-        if i * TILE % CHUNK == 0:
-            tok_copy(i * TILE // CHUNK).wait()
-            if i == 0:
-                for copy in ahead:
-                    copy.start()
-        part = pl.ds(i * TILE, TILE)
-        logits = jnp.dot(tok[part, :], keys[...], preferred_element_type=jnp.float32)
-        logits_ref[part, :] = logits
-        peak8 = jnp.maximum(peak8, jnp.max(logits.reshape(TILE // 8, 8, slots), axis=0))
-    peak = jnp.max(peak8, axis=0, keepdims=True)
-    total8 = jnp.zeros((8, slots), jnp.float32)
-    for i in range(tiles):
-        part = pl.ds(i * TILE, TILE)
-        scores = jnp.exp(logits_ref[part, :] - peak)
-        total8 = total8 + jnp.sum(scores.reshape(TILE // 8, 8, slots), axis=0)
-        wt[:, part] = scores.astype(jnp.bfloat16).T
-    total = jnp.sum(total8, axis=0, keepdims=True)
-    stats = parts_of(peak, total)
+    folded = (TILE // 8, 8, slots)
+    kinds = []
+    for chunk in range(chunks):
+        tok_copy(chunk).wait()
+        if chunk == 0:
+            for copy in ahead:
+                copy.start()
+        peak8 = jnp.full((8, slots), -jnp.inf, jnp.float32)
+        tiles = range(chunk * CHUNK // TILE, (chunk + 1) * CHUNK // TILE)
+        for i in tiles:
+            part = pl.ds(i * TILE, TILE)
+            logits = jnp.dot(tok[part, :], keys[...], preferred_element_type=jnp.float32)
+            logits_ref[part, :] = logits
+            peak8 = jnp.maximum(peak8, jnp.max(logits.reshape(folded), axis=0))
+        peak = jnp.max(peak8, axis=0, keepdims=True)
+        kinds.append((peak, tiles))
+    top = functools.reduce(jnp.maximum, [peak for peak, _ in kinds])
+    total = jnp.zeros((1, slots), jnp.float32)
+    factors = []
+    for peak, tiles in kinds:
+        total8 = jnp.zeros((8, slots), jnp.float32)
+        for i in tiles:
+            part = pl.ds(i * TILE, TILE)
+            scores = jnp.exp(logits_ref[part, :] - peak)
+            total8 = total8 + jnp.sum(scores.reshape(folded), axis=0)
+            wt[:, part] = scores.astype(jnp.bfloat16).T
+        factor = jnp.exp(peak - top)
+        total = total + factor * jnp.sum(total8, axis=0, keepdims=True)
+        factors.append(factor)
+    stats = parts_of(top, total) + factors
     stats = jnp.concatenate(stats + [jnp.zeros((LANES - len(stats), slots), jnp.float32)], axis=0)
-    for b in range(slots // LANES):
-        part = slice(b * LANES, (b + 1) * LANES)
-        whole[part, width:] = stats[:, part].T
-    for n in range(width // COLS):
-        part = pl.ds(n * COLS, COLS)
-        whole[:, part] = jnp.dot(wt[...], tok[:, part], preferred_element_type=jnp.float32)
+    columns = jnp.concatenate([stats[:, b * LANES : (b + 1) * LANES].T for b in range(slots // LANES)], axis=0)
+    whole[:, width:] = columns
+    for c in range(chunks):
+        rows_c = pl.ds(c * CHUNK, CHUNK)
+        for n in range(width // COLS):
+            part = pl.ds(n * COLS, COLS)
+            piece = jnp.dot(wt[:, rows_c], tok[rows_c, part], preferred_element_type=jnp.float32)
+            piece = piece * columns[:, 6 + c : 7 + c]
+            whole[:, part] = piece if c == 0 else whole[:, part] + piece
     core = lax.axis_index("core")
     size = slots // (CORES * groups)
     mine, other = half_rows(core, slots, groups), half_rows(1 - core, slots, groups)

time: 43.4 us -> 43.1 us (level)
  no operation moved by 1% of the time
where the time goes in v5:
time: 43.1 us; the launch traced here: 42.9 us
  blocking collectives  27.7 us (64%)
  Pallas kernels  13.1 us (30%)
  waiting for transfers between devices  1.47 us (3%)
  starting transfers between devices  0.57 us (1%)
    all_to_all x1, blocking collectives, on_device(): lax.all_to_all(message, SAME_CORE, split_axis=0, concat_axis=0, tiled=True)  16.4 us
    all_to_all x1, blocking collectives, on_device(): lax.all_to_all(copies, SAME_CORE, split_axis=0, concat_axis=0, tiled=True)  11.3 us
    pallas_call x1, Pallas kernels, experts(): pl.pallas_call(expert_kernel, out_shape=jax.ShapeDtypeStruct((peers, per_...  4.57 us
    pallas_call x1, Pallas kernels, dispatch(): pl.pallas_call(functools.partial(dispatch_kernel, groups), out_shape=(jax...  4.51 us
    pallas_call x1, Pallas kernels, mix(): pl.pallas_call(functools.partial(mix_kernel, groups), out_shape=jax.Shape...  2.8 us
    ppermute x1, waiting for transfers between devices, on_device(): other = lax.ppermute(mine, 'core', swap)  1.39 us
    pallas_call x1, Pallas kernels, combining(): pl.pallas_call(combine_kernel, out_shape=(jax.ShapeDtypeStruct(logits.sha...  0.97 us
  transfers between devices with their start and end apart: 2, of which 2 were waited for; matrix products, arithmetic and copies ran while one was open for 0% of the time, Pallas kernels for 2%

profile of v5, /device:TPU:0, one launch (start us, length us, event | category | flops | bytes accessed | tf_op | source)
XLA Modules:
  0.0 42.9 jit_solution(5699079575896117795)
XLA Ops:
  0.0 4.5 %dispatch.1 = (bf16[64,1408]{1,0:T(8,128)(2,1)S(1)}, f32[64,1408]{1,0:T(8,128)S(1)}, f32[2048,128]{1,0:T(8,128)S(1)}, f32[1,1280]{1,0:T(1,128)S(1)}, bf16[512,2560]{1,0:T(8,128)(2,1)S(1)}) custom-call(bf16[2048,1280]{1,0:T(8,128)(2,1)} %tok_hbm.1, bf16[1280,128]{1,0:T(8,128)(2,1)} %keys_hbm.1, f32[1,1280]{1,0:T(1,128)} %gain_hbm.1, ...), custom_call_target="tpu_custom_call" | custom-call | flops 1342177280 | bytes 5242880 | tf_op jit(solution)/shard_map/dispatch/pallas_call | solution.py:126
  4.5 0.6 %collective-permute-start = (bf16[64,1408]{1,0:T(8,128)(2,1)S(1)}, bf16[64,1408]{1,0:T(8,128)(2,1)S(1)}, u32[]{:S(2)}, u32[]{:S(2)}) collective-permute-start(bf16[64,1408]{1,0:T(8,128)(2,1)S(1)} %get-tuple-element.15), channel_id=1, source_target_pairs={{0,4},{4,0},{1,5},{5,1},{2,6},{6,2},{3,7},{7,3},{8,12},{12,8},{9,1... | collective-permute-start | bytes 540680 | tf_op jit(solution)/shard_map/ppermute | solution.py:340
  5.1 1.0 %combining.1 = (bf16[2048,128]{1,0:T(8,128)(2,1)S(1)}, f32[8,128]{1,0:T(8,128)S(1)}) custom-call(f32[2048,128]{1,0:T(8,128)S(1)} %get-tuple-element.12.logits_ref), custom_call_target="tpu_custom_call" | custom-call | flops 2097152 | bytes 1572864 | tf_op jit(solution)/shard_map/combining/pallas_call | solution.py:200
  6.1 0.1 collective-permute-done.got_ref
  6.1 0.3 merge.1
  6.4 16.4 %all_to_all.10.recv_ref = bf16[16,4,1408]{2,1,0:T(4,128)(2,1)S(1)} all-to-all(bf16[16,4,1408]{2,1,0:T(4,128)(2,1)S(1)} %merge.1), channel_id=1, replica_groups=mesh['far'=4,'core'=2,'grp'=4] {'far','grp'}, dimensions={0} | all-to-all | bytes 360448 | tf_op jit(solution)/shard_map/all_to_all | solution.py:343
  22.8 4.6 %experts.1 = bf16[16,4,1280]{2,1,0:T(4,128)(2,1)S(1)} custom-call(bf16[16,4,1408]{2,1,0:T(4,128)(2,1)S(1)} %all_to_all.10.recv_ref, f32[1,1280]{1,0:T(1,128)S(1)} %get-tuple-element.17.gain_ref, bf16[512,2560]{1,0:T(8,128)(2,1)S(1)} %get-tuple-element.18.head_ref, bf16[1,1280,2560]{2,1,0:T(8,128)(2,1)} %w_in_hbm.3, bf16[1,2560,1280]{2,1,0:T(8,128)(2,1)} %w_out_hbm.1), custom_call_target="tpu_custom_call" | custom-call | flops 52428800 | bytes 13107200 | tf_op jit(solution)/shard_map/experts/pallas_call | solution.py:271
  27.4 11.3 %all_to_all.11.mine_ref = bf16[16,4,1280]{2,1,0:T(4,128)(2,1)S(1)} all-to-all(bf16[16,4,1280]{2,1,0:T(4,128)(2,1)S(1)} %experts.1), channel_id=1, replica_groups=mesh['far'=4,'core'=2,'grp'=4] {'far','grp'}, dimensions={0} | all-to-all | bytes 327680 | tf_op jit(solution)/shard_map/all_to_all | solution.py:345
  38.7 0.0 collective-permute-start.1
  38.7 1.4 %collective-permute-done.1.other_ref = bf16[16,4,1280]{2,1,0:T(4,128)(2,1)S(1)} collective-permute-done((bf16[16,4,1280]{2,1,0:T(4,128)(2,1)S(1)}, bf16[16,4,1280]{2,1,0:T(4,128)(2,1)S(1)}, u32[]{:S(2)}, u32[]{:S(2)}) %collective-permute-start.1) | collective-permute-done | bytes 163872 | tf_op jit(solution)/shard_map/ppermute | solution.py:346
  40.1 2.8 %mix.1 = bf16[2048,1280]{1,0:T(8,128)(2,1)} custom-call(bf16[2048,128]{1,0:T(8,128)(2,1)S(1)} %get-tuple-element.13.combine_ref, bf16[16,4,1280]{2,1,0:T(4,128)(2,1)S(1)} %all_to_all.11.mine_ref, bf16[16,4,1280]{2,1,0:T(4,128)(2,1)S(1)} %collective-permute-done.1.other_ref), custom_call_target="tpu_custom_call" | custom-call | flops 671088640 | bytes 5242880 | tf_op jit(solution)/shard_map/mix/pallas_call | solution.py:317
Async XLA Ops:
  4.5 1.6 %collective-permute-start = (bf16[64,1408]{1,0:T(8,128)(2,1)S(1)}, bf16[64,1408]{1,0:T(8,128)(2,1)S(1)}, u32[]{:S(2)}, u32[]{:S(2)}) collective-permute-start(bf16[64,1408]{1,0:T(8,128)(2,1)S(1)} %get-tuple-element.15), channel_id=1, source_target_pairs={{0,4},{4,0},{1,5},{5,1},{2,6},{6,2},{3,7},{7,3},{8,12},{12,8},{9,1... | collective-permute-start | bytes 540680 | tf_op jit(solution)/shard_map/ppermute | solution.py:340
  38.7 1.4 %collective-permute-start.1 = (bf16[16,4,1280]{2,1,0:T(4,128)(2,1)S(1)}, bf16[16,4,1280]{2,1,0:T(4,128)(2,1)S(1)}, u32[]{:S(2)}, u32[]{:S(2)}) collective-permute-start(bf16[16,4,1280]{2,1,0:T(4,128)(2,1)S(1)} %all_to_all.11.mine_ref), channel_id=1, source_target_pairs={{0,4},{4,0},{1,5},{5,1},{2,6},{6,2},{3,7},{7,3},{8,12},{12,8},{9,1... | collective-permute-start | bytes 491528 | tf_op jit(solution)/shard_map/ppermute | solution.py:346

commit v6 on v5

--- a/solution.py
+++ b/solution.py
@@ -13,8 +13,8 @@
 LANES = 128
 TILE = 256
 COLS = 256
-HEAD = 512
-IN_CHUNKS = (384, 384)
+HEAD = 1024
+IN_CHUNKS = (128, 128)
 OUT_CHUNKS = (768, 768, 640, 384)
 STARTS = (4, 2)
 CHUNK = 1024

time: 43.1 us -> 42.3 us (0.981)
  Pallas kernels: 13.1 us -> 12.4 us
    pallas_call x1, Pallas kernels: 4.57 us -> 3.8 us  [experts(): pl.pallas_call(expert_kernel, out_shape=jax.ShapeDtypeStruct((peers, per_...]
where the time goes in v6:
time: 42.3 us; the launch traced here: 42.1 us
  blocking collectives  27.7 us (65%)
  Pallas kernels  12.4 us (29%)
  waiting for transfers between devices  1.47 us (3%)
  starting transfers between devices  0.57 us (1%)
    all_to_all x1, blocking collectives, on_device(): lax.all_to_all(message, SAME_CORE, split_axis=0, concat_axis=0, tiled=True)  16.4 us
    all_to_all x1, blocking collectives, on_device(): lax.all_to_all(copies, SAME_CORE, split_axis=0, concat_axis=0, tiled=True)  11.3 us
    pallas_call x1, Pallas kernels, dispatch(): pl.pallas_call(functools.partial(dispatch_kernel, groups), out_shape=(jax...  4.51 us
    pallas_call x1, Pallas kernels, experts(): pl.pallas_call(expert_kernel, out_shape=jax.ShapeDtypeStruct((peers, per_...  3.8 us
    pallas_call x1, Pallas kernels, mix(): pl.pallas_call(functools.partial(mix_kernel, groups), out_shape=jax.Shape...  2.8 us
    ppermute x1, waiting for transfers between devices, on_device(): other = lax.ppermute(mine, 'core', swap)  1.39 us
    pallas_call x1, Pallas kernels, combining(): pl.pallas_call(combine_kernel, out_shape=(jax.ShapeDtypeStruct(logits.sha...  0.97 us
  transfers between devices with their start and end apart: 2, of which 2 were waited for; matrix products, arithmetic and copies ran while one was open for 0% of the time, Pallas kernels for 2%

profile of v6, /device:TPU:0, one launch (start us, length us, event | category | flops | bytes accessed | tf_op | source)
XLA Modules:
  0.0 42.1 jit_solution(8644307802720428251)
XLA Ops:
  0.0 4.5 %dispatch.1 = (bf16[64,1408]{1,0:T(8,128)(2,1)S(1)}, f32[64,1408]{1,0:T(8,128)S(1)}, f32[2048,128]{1,0:T(8,128)S(1)}, f32[1,1280]{1,0:T(1,128)S(1)}, bf16[1024,2560]{1,0:T(8,128)(2,1)S(1)}) custom-call(bf16[2048,1280]{1,0:T(8,128)(2,1)} %tok_hbm.1, bf16[1280,128]{1,0:T(8,128)(2,1)} %keys_hbm.1, f32[1,1280]{1,0:T(1,128)} %gain_hbm.1, ...), custom_call_target="tpu_custom_call" | custom-call | flops 1342177280 | bytes 5242880 | tf_op jit(solution)/shard_map/dispatch/pallas_call | solution.py:126
  4.5 0.6 %collective-permute-start = (bf16[64,1408]{1,0:T(8,128)(2,1)S(1)}, bf16[64,1408]{1,0:T(8,128)(2,1)S(1)}, u32[]{:S(2)}, u32[]{:S(2)}) collective-permute-start(bf16[64,1408]{1,0:T(8,128)(2,1)S(1)} %get-tuple-element.15), channel_id=1, source_target_pairs={{0,4},{4,0},{1,5},{5,1},{2,6},{6,2},{3,7},{7,3},{8,12},{12,8},{9,1... | collective-permute-start | bytes 540680 | tf_op jit(solution)/shard_map/ppermute | solution.py:340
  5.1 1.0 %combining.1 = (bf16[2048,128]{1,0:T(8,128)(2,1)S(1)}, f32[8,128]{1,0:T(8,128)S(1)}) custom-call(f32[2048,128]{1,0:T(8,128)S(1)} %get-tuple-element.12.logits_ref), custom_call_target="tpu_custom_call" | custom-call | flops 2097152 | bytes 1572864 | tf_op jit(solution)/shard_map/combining/pallas_call | solution.py:200
  6.1 0.1 collective-permute-done.got_ref
  6.1 0.3 merge.1
  6.4 16.4 %all_to_all.10.recv_ref = bf16[16,4,1408]{2,1,0:T(4,128)(2,1)S(1)} all-to-all(bf16[16,4,1408]{2,1,0:T(4,128)(2,1)S(1)} %merge.1), channel_id=1, replica_groups=mesh['far'=4,'core'=2,'grp'=4] {'far','grp'}, dimensions={0} | all-to-all | bytes 360448 | tf_op jit(solution)/shard_map/all_to_all | solution.py:343
  22.8 3.8 %experts.1 = bf16[16,4,1280]{2,1,0:T(4,128)(2,1)S(1)} custom-call(bf16[16,4,1408]{2,1,0:T(4,128)(2,1)S(1)} %all_to_all.10.recv_ref, f32[1,1280]{1,0:T(1,128)S(1)} %get-tuple-element.17.gain_ref, bf16[1024,2560]{1,0:T(8,128)(2,1)S(1)} %get-tuple-element.18.head_ref, bf16[1,1280,2560]{2,1,0:T(8,128)(2,1)} %w_in_hbm.3, bf16[1,2560,1280]{2,1,0:T(8,128)(2,1)} %w_out_hbm.1), custom_call_target="tpu_custom_call" | custom-call | flops 52428800 | bytes 13107200 | tf_op jit(solution)/shard_map/experts/pallas_call | solution.py:271
  26.6 11.3 %all_to_all.11.mine_ref = bf16[16,4,1280]{2,1,0:T(4,128)(2,1)S(1)} all-to-all(bf16[16,4,1280]{2,1,0:T(4,128)(2,1)S(1)} %experts.1), channel_id=1, replica_groups=mesh['far'=4,'core'=2,'grp'=4] {'far','grp'}, dimensions={0} | all-to-all | bytes 327680 | tf_op jit(solution)/shard_map/all_to_all | solution.py:345
  37.9 0.0 collective-permute-start.1
  37.9 1.4 %collective-permute-done.1.other_ref = bf16[16,4,1280]{2,1,0:T(4,128)(2,1)S(1)} collective-permute-done((bf16[16,4,1280]{2,1,0:T(4,128)(2,1)S(1)}, bf16[16,4,1280]{2,1,0:T(4,128)(2,1)S(1)}, u32[]{:S(2)}, u32[]{:S(2)}) %collective-permute-start.1) | collective-permute-done | bytes 163872 | tf_op jit(solution)/shard_map/ppermute | solution.py:346
  39.3 2.8 %mix.1 = bf16[2048,1280]{1,0:T(8,128)(2,1)} custom-call(bf16[2048,128]{1,0:T(8,128)(2,1)S(1)} %get-tuple-element.13.combine_ref, bf16[16,4,1280]{2,1,0:T(4,128)(2,1)S(1)} %all_to_all.11.mine_ref, bf16[16,4,1280]{2,1,0:T(4,128)(2,1)S(1)} %collective-permute-done.1.other_ref), custom_call_target="tpu_custom_call" | custom-call | flops 671088640 | bytes 5242880 | tf_op jit(solution)/shard_map/mix/pallas_call | solution.py:317
Async XLA Ops:
  4.5 1.6 %collective-permute-start = (bf16[64,1408]{1,0:T(8,128)(2,1)S(1)}, bf16[64,1408]{1,0:T(8,128)(2,1)S(1)}, u32[]{:S(2)}, u32[]{:S(2)}) collective-permute-start(bf16[64,1408]{1,0:T(8,128)(2,1)S(1)} %get-tuple-element.15), channel_id=1, source_target_pairs={{0,4},{4,0},{1,5},{5,1},{2,6},{6,2},{3,7},{7,3},{8,12},{12,8},{9,1... | collective-permute-start | bytes 540680 | tf_op jit(solution)/shard_map/ppermute | solution.py:340
  37.9 1.4 %collective-permute-start.1 = (bf16[16,4,1280]{2,1,0:T(4,128)(2,1)S(1)}, bf16[16,4,1280]{2,1,0:T(4,128)(2,1)S(1)}, u32[]{:S(2)}, u32[]{:S(2)}) collective-permute-start(bf16[16,4,1280]{2,1,0:T(4,128)(2,1)S(1)} %all_to_all.11.mine_ref), channel_id=1, source_target_pairs={{0,4},{4,0},{1,5},{5,1},{2,6},{6,2},{3,7},{7,3},{8,12},{12,8},{9,1... | collective-permute-start | bytes 491528 | tf_op jit(solution)/shard_map/ppermute | solution.py:346

commit v7 on v6

--- a/solution.py
+++ b/solution.py
@@ -13,8 +13,8 @@
 LANES = 128
 TILE = 256
 COLS = 256
-HEAD = 1024
-IN_CHUNKS = (128, 128)
+HEAD = 1152
+IN_CHUNKS = (64, 64)
 OUT_CHUNKS = (768, 768, 640, 384)
 STARTS = (4, 2)
 CHUNK = 1024
@@ -68,13 +68,12 @@
         pltpu.make_async_copy(gain_hbm, gain_ref, head_sem.at[0]),
         pltpu.make_async_copy(w_in_hbm.at[0, pl.ds(0, HEAD)], head_ref, head_sem.at[1]),
     )
+    for copy in ahead:
+        copy.start()
     folded = (TILE // 8, 8, slots)
     kinds = []
     for chunk in range(chunks):
         tok_copy(chunk).wait()
-        if chunk == 0:
-            for copy in ahead:
-                copy.start()
         peak8 = jnp.full((8, slots), -jnp.inf, jnp.float32)
         tiles = range(chunk * CHUNK // TILE, (chunk + 1) * CHUNK // TILE)
         for i in tiles:
@@ -156,7 +155,7 @@
 def merge_kernel(keep_ref, got_ref, ready_ref, msg_ref):
     peers, per_dev, wide = msg_ref.shape
     width = wide - LANES
-    size = 16
+    size = 32
     lane = lax.broadcasted_iota(jnp.int32, (size, LANES), 1)
     for b in range(keep_ref.shape[0] // size):
         rows = pl.ds(b * size, size)
@@ -289,6 +288,23 @@
     )(recv, gain, head, in_hbm(w_in), in_hbm(w_out))
 
 
+def flatten_kernel(rows_ref, flat_ref):
+    flat_ref[...] = rows_ref[...].reshape(flat_ref.shape)
+
+
+def flatten(rows):
+    shape = (rows.shape[0] * rows.shape[1], rows.shape[2])
+    return pl.pallas_call(
+        flatten_kernel,
+        out_shape=jax.ShapeDtypeStruct(shape, rows.dtype),
+        in_specs=[pl.BlockSpec(memory_space=pltpu.VMEM)],
+        out_specs=pl.BlockSpec(memory_space=pltpu.VMEM),
+        name="flatten",
+        compiler_params=pltpu.CompilerParams(vmem_limit_bytes=16 << 20),
+        cost_estimate=pl.CostEstimate(flops=rows.size, bytes_accessed=4 * rows.size, transcendentals=0),
+    )(rows)
+
+
 def mix_kernel(groups, combine_ref, mine_ref, other_ref, out_hbm, table, out, sems):
     rows, width = out.shape
     slots = table.shape[0]
@@ -313,7 +329,7 @@
 
 def mix(groups, combine, mine, other):
     rows, slots = combine.shape
-    width = mine.shape[2]
+    width = mine.shape[1]
     return pl.pallas_call(
         functools.partial(mix_kernel, groups),
         out_shape=jax.ShapeDtypeStruct((rows, width), jnp.bfloat16),
@@ -344,7 +360,7 @@
     copies = experts(received, gain, head, w_in, w_out)
     mine = lax.all_to_all(copies, SAME_CORE, split_axis=0, concat_axis=0, tiled=True)
     other = lax.ppermute(mine, "core", swap)
-    return mix(groups, combine, mine, other)
+    return mix(groups, combine, flatten(mine), other)
 
 
 def solution(mesh):

time: 42.3 us -> 42.3 us (level)
  no operation moved by 1% of the time
where the time goes in v7:
time: 42.3 us; the launch traced here: 42.1 us
  blocking collectives  27.7 us (65%)
  Pallas kernels  12.3 us (29%)
  waiting for transfers between devices  1.44 us (3%)
  starting transfers between devices  0.56 us (1%)
    all_to_all x1, blocking collectives, on_device(): lax.all_to_all(message, SAME_CORE, split_axis=0, concat_axis=0, tiled=True)  16.4 us
    all_to_all x1, blocking collectives, on_device(): lax.all_to_all(copies, SAME_CORE, split_axis=0, concat_axis=0, tiled=True)  11.3 us
    pallas_call x1, Pallas kernels, dispatch(): pl.pallas_call(functools.partial(dispatch_kernel, groups), out_shape=(jax...  4.68 us
    pallas_call x1, Pallas kernels, experts(): pl.pallas_call(expert_kernel, out_shape=jax.ShapeDtypeStruct((peers, per_...  3.61 us
    pallas_call x1, Pallas kernels, mix(): pl.pallas_call(functools.partial(mix_kernel, groups), out_shape=jax.Shape...  2.79 us
    ppermute x1, waiting for transfers between devices, on_device(): other = lax.ppermute(mine, 'core', swap)  1.37 us
    pallas_call x1, Pallas kernels, combining(): pl.pallas_call(combine_kernel, out_shape=(jax.ShapeDtypeStruct(logits.sha...  0.97 us
  transfers between devices with their start and end apart: 2, of which 2 were waited for; matrix products, arithmetic and copies ran while one was open for 0% of the time, Pallas kernels for 2%

profile of v7, /device:TPU:0, one launch (start us, length us, event | category | flops | bytes accessed | tf_op | source)
XLA Modules:
  0.0 42.1 jit_solution(14224627775586839490)
XLA Ops:
  0.0 4.7 %dispatch.1 = (bf16[64,1408]{1,0:T(8,128)(2,1)S(1)}, f32[64,1408]{1,0:T(8,128)S(1)}, f32[2048,128]{1,0:T(8,128)S(1)}, f32[1,1280]{1,0:T(1,128)S(1)}, bf16[1152,2560]{1,0:T(8,128)(2,1)S(1)}) custom-call(bf16[2048,1280]{1,0:T(8,128)(2,1)} %tok_hbm.1, bf16[1280,128]{1,0:T(8,128)(2,1)} %keys_hbm.1, f32[1,1280]{1,0:T(1,128)} %gain_hbm.1, ...), custom_call_target="tpu_custom_call" | custom-call | flops 1342177280 | bytes 5242880 | tf_op jit(solution)/shard_map/dispatch/pallas_call | solution.py:125
  4.7 0.6 %collective-permute-start = (bf16[64,1408]{1,0:T(8,128)(2,1)S(1)}, bf16[64,1408]{1,0:T(8,128)(2,1)S(1)}, u32[]{:S(2)}, u32[]{:S(2)}) collective-permute-start(bf16[64,1408]{1,0:T(8,128)(2,1)S(1)} %get-tuple-element.15), channel_id=1, source_target_pairs={{0,4},{4,0},{1,5},{5,1},{2,6},{6,2},{3,7},{7,3},{8,12},{12,8},{9,1... | collective-permute-start | bytes 540680 | tf_op jit(solution)/shard_map/ppermute | solution.py:356
  5.2 1.0 %combining.1 = (bf16[2048,128]{1,0:T(8,128)(2,1)S(1)}, f32[8,128]{1,0:T(8,128)S(1)}) custom-call(f32[2048,128]{1,0:T(8,128)S(1)} %get-tuple-element.12.logits_ref), custom_call_target="tpu_custom_call" | custom-call | flops 2097152 | bytes 1572864 | tf_op jit(solution)/shard_map/combining/pallas_call | solution.py:199
  6.2 0.1 collective-permute-done.got_ref
  6.3 0.3 merge.1
  6.6 16.4 %all_to_all.10.recv_ref = bf16[16,4,1408]{2,1,0:T(4,128)(2,1)S(1)} all-to-all(bf16[16,4,1408]{2,1,0:T(4,128)(2,1)S(1)} %merge.1), channel_id=1, replica_groups=mesh['far'=4,'core'=2,'grp'=4] {'far','grp'}, dimensions={0} | all-to-all | bytes 360448 | tf_op jit(solution)/shard_map/all_to_all | solution.py:359
  23.0 3.6 %experts.1 = bf16[16,4,1280]{2,1,0:T(4,128)(2,1)S(1)} custom-call(bf16[16,4,1408]{2,1,0:T(4,128)(2,1)S(1)} %all_to_all.10.recv_ref, f32[1,1280]{1,0:T(1,128)S(1)} %get-tuple-element.17.gain_ref, bf16[1152,2560]{1,0:T(8,128)(2,1)S(1)} %get-tuple-element.18.head_ref, bf16[1,1280,2560]{2,1,0:T(8,128)(2,1)} %w_in_hbm.3, bf16[1,2560,1280]{2,1,0:T(8,128)(2,1)} %w_out_hbm.1), custom_call_target="tpu_custom_call" | custom-call | flops 52428800 | bytes 13107200 | tf_op jit(solution)/shard_map/experts/pallas_call | solution.py:270
  26.6 11.3 %all_to_all.11.rows_ref = bf16[16,4,1280]{2,1,0:T(4,128)(2,1)S(1)} all-to-all(bf16[16,4,1280]{2,1,0:T(4,128)(2,1)S(1)} %experts.1), channel_id=1, replica_groups=mesh['far'=4,'core'=2,'grp'=4] {'far','grp'}, dimensions={0} | all-to-all | bytes 327680 | tf_op jit(solution)/shard_map/all_to_all | solution.py:361
  37.9 0.0 collective-permute-start.1
  37.9 1.4 %collective-permute-done.1.other_ref = bf16[16,4,1280]{2,1,0:T(4,128)(2,1)S(1)} collective-permute-done((bf16[16,4,1280]{2,1,0:T(4,128)(2,1)S(1)}, bf16[16,4,1280]{2,1,0:T(4,128)(2,1)S(1)}, u32[]{:S(2)}, u32[]{:S(2)}) %collective-permute-start.1) | collective-permute-done | bytes 163872 | tf_op jit(solution)/shard_map/ppermute | solution.py:362
  39.3 2.8 %mix.1 = bf16[2048,1280]{1,0:T(8,128)(2,1)} custom-call(bf16[2048,128]{1,0:T(8,128)(2,1)S(1)} %get-tuple-element.13.combine_ref, bf16[64,1280]{1,0:T(8,128)(2,1)S(1)} %flatten.1.mine_ref, bf16[16,4,1280]{2,1,0:T(4,128)(2,1)S(1)} %collective-permute-done.1.other_ref), custom_call_target="tpu_custom_call" | custom-call | flops 671088640 | bytes 5242880 | tf_op jit(solution)/shard_map/mix/pallas_call | solution.py:333
  (1 shorter events, 0.0 us)
Async XLA Ops:
  4.7 1.6 %collective-permute-start = (bf16[64,1408]{1,0:T(8,128)(2,1)S(1)}, bf16[64,1408]{1,0:T(8,128)(2,1)S(1)}, u32[]{:S(2)}, u32[]{:S(2)}) collective-permute-start(bf16[64,1408]{1,0:T(8,128)(2,1)S(1)} %get-tuple-element.15), channel_id=1, source_target_pairs={{0,4},{4,0},{1,5},{5,1},{2,6},{6,2},{3,7},{7,3},{8,12},{12,8},{9,1... | collective-permute-start | bytes 540680 | tf_op jit(solution)/shard_map/ppermute | solution.py:356
  37.9 1.4 %collective-permute-start.1 = (bf16[16,4,1280]{2,1,0:T(4,128)(2,1)S(1)}, bf16[16,4,1280]{2,1,0:T(4,128)(2,1)S(1)}, u32[]{:S(2)}, u32[]{:S(2)}) collective-permute-start(bf16[16,4,1280]{2,1,0:T(4,128)(2,1)S(1)} %all_to_all.11.rows_ref), channel_id=1, source_target_pairs={{0,4},{4,0},{1,5},{5,1},{2,6},{6,2},{3,7},{7,3},{8,12},{12,8},{9,1... | collective-permute-start | bytes 491528 | tf_op jit(solution)/shard_map/ppermute | solution.py:362
